TPU v7x, 512 devices: a whole 4x4x16 slice. The times are simulated.
512 devices in a mesh: dp: 64 (over y_lo, z, core), blk: 8 (over y_hi, x).
Axes of the slice: x: 4, y: 4 (y_hi: 2, y_lo: 2; y = y_hi * 2 + y_lo), z: 16, core: 2. Of those that a mesh axis runs over, the one named last changes fastest.
Arguments:
- resid: bfloat16 [2048, 2048], P('dp'), may hold values from -40 to 40
- queries: bfloat16 [2048, 16, 128], P('dp', 'blk'), may hold values from -60 to 60
- new_kv: bfloat16 [2048, 2, 8, 128], P('dp', None, 'blk'), may hold values from -6 to 6
- prefix_pool: bfloat16 [2048, 128, 2, 8, 128], P('dp', None, None, 'blk'), may hold values from -6 to 6
- page_table: int32 [64, 32], P('dp'), may hold values from 0 to 31, each once within a row
- prompt_len: int32 [64], P('dp'), may hold values from 1 to 4096, 131072 in all
- tail_pool: bfloat16 [1024, 128, 2, 8, 128], P('dp', None, None, 'blk'), may hold values from -6 to 6
- tail_len: int32 [64, 16], P('dp'), may hold values from 1 to 128, 1024 in all within a row
- migration: int32 [1024], replicated, may hold values from 0 to 1023, each once
- out_w: bfloat16 [2048, 2048], P('blk'), may hold values from -0.125 to 0.125
- mlp_gain: bfloat16 [2048], replicated, may hold values from 0.099609375 to 1.8984375
- gate_w: bfloat16 [2048, 6144], P('blk', 'dp'), may hold values from -0.125 to 0.125
- up_w: bfloat16 [2048, 6144], P('blk', 'dp'), may hold values from -0.125 to 0.125
- down_w: bfloat16 [6144, 2048], P('dp', 'blk'), may hold values from -0.078125 to 0.078125
- final_gain: bfloat16 [2048], P('blk'), may hold values from 0.099609375 to 1.8984375
- score_w: bfloat16 [2048], P('blk'), may hold values from -0.125 to 0.125
Outputs:
- hidden_out: bfloat16 [2048, 2048], P('dp', 'blk')
- score: float32 [2048], P('dp')
Inputs may be any that keep to these rules, and one draw needn't show every extreme that they name: `page_table`: each row lists every page of the device's pool once. `migration`: names every continuation once.
All inputs are finite; a program needn't handle non-finite values. No bound on the sum of `prompt_len` on one device may be relied on, other than what follows from the above.
Results may differ from a plain program's by a relative error of at most 0.012.
Values may be sent and summed in bfloat16 or wider, within the bound.
A program may use at most 64 MiB of HBM per device.

v0:
```python
import math

import jax
import jax.numpy as jnp
from jax import lax
from jax.sharding import PartitionSpec as P

D = 2048
NEW = 2


NEG = -1e30
EPS = 1e-06


def attend_prompt(queries, pool, table, prompt_len, tails, tail_len, pairs):
    token_rows, heads, width = queries.shape
    groups = pairs.shape[2]
    repeat = heads // groups
    conts = tails.shape[0]
    fresh = token_rows // conts
    prefix = jnp.take(pool, table, axis=0).reshape(-1, 2, groups, width)
    span = prefix.shape[0]
    grouped = queries.reshape(conts, fresh, groups, repeat, width)
    recent = pairs.reshape(conts, fresh, 2, groups, width)
    factor = 1.0 / math.sqrt(width)
    pre_scores = (
        jnp.einsum("cngrd,pgd->gcnrp", grouped, prefix[:, 0], preferred_element_type=jnp.float32)
        * factor
    )
    tail_scores = (
        jnp.einsum("cngrd,ctgd->gcnrt", grouped, tails[:, :, 0], preferred_element_type=jnp.float32)
        * factor
    )
    new_scores = (
        jnp.einsum(
            "cngrd,cmgd->gcnrm", grouped, recent[:, :, 0], preferred_element_type=jnp.float32
        )
        * factor
    )
    pre_mask = (jnp.arange(span) < prompt_len)[None, None, None, None, :]
    tail_mask = (jnp.arange(tails.shape[1])[None, :] < tail_len[:, None])[None, :, None, None, :]
    new_mask = (jnp.arange(fresh)[None, :] <= jnp.arange(fresh)[:, None])[None, None, :, None, :]
    pre_scores = jnp.where(pre_mask, pre_scores, NEG)
    tail_scores = jnp.where(tail_mask, tail_scores, NEG)
    new_scores = jnp.where(new_mask, new_scores, NEG)
    highest = jnp.maximum(
        jnp.maximum(jnp.max(pre_scores, -1), jnp.max(tail_scores, -1)), jnp.max(new_scores, -1)
    )[..., None]
    pre_weights = jnp.where(pre_mask, jnp.exp(pre_scores - highest), 0.0)
    tail_weights = jnp.where(tail_mask, jnp.exp(tail_scores - highest), 0.0)
    new_weights = jnp.where(new_mask, jnp.exp(new_scores - highest), 0.0)
    total = jnp.sum(pre_weights, -1) + jnp.sum(tail_weights, -1) + jnp.sum(new_weights, -1)
    mixed = jnp.einsum(
        "gcnrp,pgd->cngrd",
        pre_weights.astype(jnp.bfloat16),
        prefix[:, 1],
        preferred_element_type=jnp.float32,
    )
    mixed = mixed + jnp.einsum(
        "gcnrt,ctgd->cngrd",
        tail_weights.astype(jnp.bfloat16),
        tails[:, :, 1],
        preferred_element_type=jnp.float32,
    )
    mixed = mixed + jnp.einsum(
        "gcnrm,cmgd->cngrd",
        new_weights.astype(jnp.bfloat16),
        recent[:, :, 1],
        preferred_element_type=jnp.float32,
    )
    mixed = mixed / jnp.transpose(total, (1, 2, 0, 3))[..., None]
    return mixed.reshape(token_rows, heads * width).astype(jnp.bfloat16)


def shards(
    resid,
    queries,
    new_kv,
    prefix_pool,
    page_table,
    prompt_len,
    tail_pool,
    tail_len,
    migration,
    out_w,
    mlp_gain,
    gate_w,
    up_w,
    down_w,
    final_gain,
    score_w,
):
    token_rows = resid.shape[0]
    attn = attend_prompt(
        queries, prefix_pool, page_table[0], prompt_len[0], tail_pool, tail_len[0], new_kv
    )
    partial_value = jnp.dot(attn, out_w, preferred_element_type=jnp.float32)
    mixed = lax.psum(partial_value.astype(jnp.bfloat16), "blk").astype(jnp.float32)
    middle = resid.astype(jnp.float32) + mixed
    normed = (
        middle
        * lax.rsqrt(jnp.mean(middle * middle, -1, keepdims=True) + EPS)
        * mlp_gain.astype(jnp.float32)
    ).astype(jnp.bfloat16)
    feat_width = gate_w.shape[0]
    units = gate_w.shape[1]
    block_index = lax.axis_index("blk")
    home_index = lax.axis_index("dp")
    feat_slice = lax.dynamic_slice_in_dim(normed, block_index * feat_width, feat_width, 1)
    middle_slice = lax.dynamic_slice_in_dim(middle, block_index * feat_width, feat_width, 1)
    piece = lax.all_gather(feat_slice, "dp", axis=0, tiled=True)
    partial_units = jnp.concatenate(
        [
            jnp.dot(piece, gate_w, preferred_element_type=jnp.float32),
            jnp.dot(piece, up_w, preferred_element_type=jnp.float32),
        ],
        axis=1,
    )
    summed = lax.psum(partial_units.astype(jnp.bfloat16), "blk").astype(jnp.float32)
    hidden = (jax.nn.silu(summed[:, :units]) * summed[:, units:]).astype(jnp.bfloat16)
    source = (migration[:, None] * NEW + jnp.arange(NEW, dtype=jnp.int32)[None, :]).reshape(-1)
    term = jnp.dot(jnp.take(hidden, source, axis=0), down_w, preferred_element_type=jnp.float32)
    local_rows = source - home_index * token_rows
    own_rows = (local_rows >= 0) & (local_rows < token_rows)
    carried = jnp.take(middle_slice, jnp.clip(local_rows, 0, token_rows - 1), axis=0)
    moved = lax.psum_scatter(
        term + jnp.where(own_rows[:, None], carried, 0.0), "dp", scatter_dimension=0, tiled=True
    )
    weighted = final_gain.astype(jnp.float32) * score_w.astype(jnp.float32)
    squares, terms = lax.psum((jnp.sum(moved * moved, -1), jnp.sum(moved * weighted, -1)), "blk")
    score = terms * lax.rsqrt(squares / D + EPS)
    return (moved.astype(jnp.bfloat16), score)


def solution(mesh):
    return jax.shard_map(
        shards,
        mesh=mesh,
        in_specs=(
            P("dp", None),
            P("dp", "blk", None),
            P("dp", None, "blk", None),
            P("dp", None, None, "blk", None),
            P("dp", None),
            P("dp"),
            P("dp", None, None, "blk", None),
            P("dp", None),
            P(),
            P("blk", None),
            P(),
            P("blk", "dp"),
            P("blk", "dp"),
            P("dp", "blk"),
            P("blk"),
            P("blk"),
        ),
        out_specs=(P("dp", "blk"), P("dp")),
        check_vma=False,
    )
```

profile of v0, /device:TPU:24, one launch (start us, length us, event | category | flops | bytes accessed | tf_op | source)
XLA Modules:
  0.0 630.5 jit_solution(11279439814743314583)
XLA Ops:
  7.2 0.0 copy-start
  7.2 0.0 all-reduce.4.cloned.1.call-start
  7.2 0.8 fusion.25
  8.0 0.7 compare_and_fusion.3
  9.4 6.2 gather_fusion
  15.5 3.6 copy.69
  19.1 0.1 broadcast_bitcast_fusion
  19.2 0.1 iota_compare_fusion.1
  19.3 0.0 copy-start.9
  19.3 2.3 fusion.31
  21.6 0.5 fusion.33
  22.1 0.1 copy.72
  22.2 0.4 fusion.22
  22.6 0.1 copy.74
  22.7 2.0 broadcast_select_fusion
  24.7 1.3 copy-done.2
  26.0 0.6 fusion.32
  26.6 0.1 fusion.24
  26.7 0.1 copy.77
  26.8 0.1 fusion.30
  26.9 0.2 fusion.26
  27.1 0.1 copy.82
  27.2 0.4 copy-done.4
  27.6 0.3 fusion.7
  27.9 1.6 fusion.11
  29.5 0.1 copy.80
  29.6 0.2 fusion.23
  29.8 0.0 copy-start.5
  29.8 0.0 copy-start.10
  29.8 1.9 fusion.6
  31.8 0.0 copy-start.7
  31.8 0.9 convolution_convert_fusion.2
  32.8 0.0 all-reduce.4.cloned.1.call-update
  32.8 0.0 all-gather.2.cloned.1.call-start
  32.9 0.8 dynamic-slice
  33.6 101.2 %all-reduce.4.cloned.1.call-done = bf16[32,2048]{1,0:T(8,128)(2,1)} async-done(((bf16[32,2048]{1,0:T(8,128)(2,1)}), bf16[32,2048]{1,0:T(8,128)(2,1)}) %all-reduce.4.cloned.1.call-update) | async-done | bytes 131088 | tf_op jit(solution)/shard_map/psum | solution.py:99
  134.9 1.1 convert_add_fusion
  135.9 0.7 multiply_convert_fusion
  136.6 0.0 all-gather.2.cloned.1.call-update
  136.6 0.0 all-reduce.6.cloned.1.call-start
  136.7 0.2 iota_add_fusion
  136.9 0.3 add.179
  137.2 0.3 add.163
  137.5 120.2 %all-gather.2.cloned.1.call-done = bf16[2048,256]{1,0:T(8,128)(2,1)} async-done(((bf16[32,256]{1,0:T(8,128)(2,1)}), bf16[2048,256]{1,0:T(8,128)(2,1)}) %all-gather.2.cloned.1.call-update) | async-done | bytes 1048592 | tf_op jit(solution)/shard_map/all_gather | solution.py:112
  257.7 1.7 convolution_convert_fusion
  259.4 1.7 convolution_convert_fusion.1
  261.1 0.9 pad_maximum_fusion
  262.0 0.0 all-reduce.6.cloned.1.call-update
  262.1 0.0 reduce-scatter.2.cloned.1.call-start
  262.2 8.6 %gather_fusion.2 = f32[2048,256]{1,0:T(8,128)} fusion(f32[32,256]{1,0:T(8,128)S(1)} %get-tuple-element.7, s32[2048]{0:T(1024)S(1)} %broadcast_clamp_fusion), kind=kCustom, calls=%fused_computation.2 | custom fusion | bytes 4202496 | tf_op jit(solution)/shard_map/jit(_take)/gather | solution.py:126
  270.7 88.4 %all-reduce.6.cloned.1.call-done = bf16[2048,192]{0,1:T(8,128)(2,1)} async-done(((bf16[2048,192]{0,1:T(8,128)(2,1)}), bf16[2048,192]{0,1:T(8,128)(2,1)}) %all-reduce.6.cloned.1.call-update) | async-done | bytes 786448 | tf_op jit(solution)/shard_map/psum | solution.py:120
  359.2 1.3 convert_element_type.59
  360.5 0.2 fusion.9
  360.7 0.3 copy.86
  361.0 0.0 copy-start.6
  361.0 6.2 gather_fusion.1
  367.2 4.9 convolution_add_fusion
  372.0 0.0 reduce-scatter.2.cloned.1.call-update
  372.1 0.6 copy-done.12
  372.7 0.0 copy-done.13
  372.7 227.0 %reduce-scatter.2.cloned.1.call-done = f32[32,256]{1,0:T(8,128)} async-done(((f32[2048,256]{1,0:T(8,128)}), f32[32,256]{1,0:T(8,128)}) %reduce-scatter.2.cloned.1.call-update) | async-done | bytes 32784 | tf_op jit(solution)/shard_map/reduce_scatter | solution.py:127
  599.7 1.5 multiply_reduce_fusion.1
  601.2 22.2 %all-reduce = (f32[32]{0:T(128)S(1)}, f32[32]{0:T(128)S(1)}) all-reduce(f32[32]{0:T(128)S(1)} %get-tuple-element.3, f32[32]{0:T(128)S(1)} %get-tuple-element.2), channel_id=1, replica_groups=mesh['dp'=64,'blk'=8] {'blk'}, use_global_device_ids=true, to_apply=%region_11.12 | all-reduce | flops 64 | bytes 512 | tf_op jit(solution)/shard_map/psum | solution.py:131
  623.4 0.5 rsqrt_multiply_fusion
  (34 shorter events, 0.2 us)
Async XLA Ops:
  7.2 2.2 copy-start
  7.2 127.7 %all-reduce.4.cloned.1.call-start = ((), (), s32[]{:S(2)}) async-start(), calls=%async_computation.1 | async-start | bytes 262144 | tf_op jit(solution)/shard_map/psum | solution.py:99
  15.5 3.7 copy-start.11
  15.5 3.7 copy-start.1
  19.3 2.3 copy-start.14
  19.3 2.9 copy-start.9
  24.7 1.4 copy-start.2
  26.6 1.0 copy-start.4
  27.9 3.9 copy-start.3
  29.8 105.0 %copy-start.5 = (bf16[32,2048]{1,0:T(8,128)(2,1)S(1)}, bf16[32,2048]{1,0:T(8,128)(2,1)}, u32[]{:S(2)}) copy-start(bf16[32,2048]{1,0:T(8,128)(2,1)} %param.16) | copy-start | bytes 393220
  29.8 106.9 %copy-start.10 = (s32[1024]{0:T(1024)S(1)}, s32[1024]{0:T(1024)}, u32[]{:S(2)}) copy-start(s32[1024]{0:T(1024)} %param.24) | copy-start | bytes 12292
  31.8 226.0 %copy-start.7 = (bf16[256,96]{0,1:T(8,128)(2,1)S(1)}, bf16[256,96]{0,1:T(8,128)(2,1)}, u32[]{:S(2)}) copy-start(bf16[256,96]{0,1:T(8,128)(2,1)} %param.28) | copy-start | bytes 147460
  32.8 226.6 %copy-start.8 = (bf16[256,96]{0,1:T(8,128)(2,1)S(1)}, bf16[256,96]{0,1:T(8,128)(2,1)}, u32[]{:S(2)}) copy-start(bf16[256,96]{0,1:T(8,128)(2,1)} %param.27) | copy-start | bytes 147460
  32.8 224.9 %all-gather.2.cloned.1.call-start = ((), (), s32[]{:S(2)}) async-start(), calls=%async_computation.2 | async-start | bytes 1064960 | tf_op jit(solution)/shard_map/all_gather | solution.py:112
  136.6 222.5 %all-reduce.6.cloned.1.call-start = ((), (), s32[]{:S(2)}) async-start(), calls=%async_computation.3 | async-start | bytes 1572864 | tf_op jit(solution)/shard_map/psum | solution.py:120
  262.1 337.6 %reduce-scatter.2.cloned.1.call-start = ((), (), s32[]{:S(2)}) async-start(), calls=%async_computation.4 | async-start | bytes 2129920 | tf_op jit(solution)/shard_map/reduce_scatter | solution.py:127
  361.0 6.2 copy-start.6
  372.0 0.7 copy-start.12
  372.0 0.7 copy-start.13
Sparse Core Ops, SparseCore 0:
  32.9 101.8 all-reduce.3
  137.8 119.8 all-gather.1
  262.2 96.9 all-reduce.5
  372.2 227.4 reduce-scatter.1
where the time goes:
time: 632 us; the launch traced here: 631 us
  waiting for transfers between devices  537 us (85%)
  local copies, waits for them, and re-layouts  31.4 us (5%)
  blocking collectives  22.2 us (4%)
  between operations  14.7 us (2%)
  matrix products  14.3 us (2%)
  other arithmetic  10.8 us (2%)
    reduce_scatter x1, waiting for transfers between devices, shards(): lax.psum_scatter(term + jnp.where(own_rows[:, None], carried, 0.0), 'dp',...  227 us
    all_gather x1, waiting for transfers between devices, shards(): piece = lax.all_gather(feat_slice, 'dp', axis=0, tiled=True)  120 us
    psum x1, waiting for transfers between devices, shards(): lax.psum(partial_value.astype(jnp.bfloat16), 'blk').astype(jnp.float32)  101 us
    psum x1, waiting for transfers between devices, shards(): lax.psum(partial_units.astype(jnp.bfloat16), 'blk').astype(jnp.float32)  88.4 us
    psum x1, blocking collectives, shards(): lax.psum((jnp.sum(moved * moved, -1), jnp.sum(moved * weighted, -1)), 'blk')  22.2 us
  transfers between devices with their start and end apart: 4, of which 4 were waited for; matrix products, arithmetic and copies ran while one was open for 2% of the time, Pallas kernels for 0%

commit v1 on v0

v1 whole, which is shorter than its diff:
```python
import functools
import math

import jax
import jax.numpy as jnp
from jax import lax
from jax.experimental import pallas as pl
from jax.experimental.pallas import tpu as pltpu
from jax.sharding import PartitionSpec as P

MESH = pl.DeviceIdType.MESH
F32 = jnp.float32
BF16 = jnp.bfloat16
NEG = -1e30
EPS = 1e-06
D = 2048
NB = 8
FB = 256
HOLD = 96
CONT = 16
PAGES = 32
HD = 128


def iota(shape, dim):
    return lax.broadcasted_iota(jnp.int32, shape, dim)


def dot(a, b):
    return lax.dot_general(a, b, (((1,), (0,)), ((), ())), preferred_element_type=F32)


def dot_nt(a, b):
    return lax.dot_general(a, b, (((1,), (1,)), ((), ())), preferred_element_type=F32)


def onehot(cond):
    return jnp.where(cond, 1.0, 0.0).astype(BF16)


def kernel(
    nz,
    radix,
    *refs,
):
    sources, (out_ref, score_ref), held, refs = refs[:16], refs[16:18], refs[18:34], refs[34:]
    (kv, tail, q_ref, new_ref, tab_ref, plen_ref, tlen_ref, down_ref, ow, resid_ref, mig_ref, gate_ref, up_ref, gain_ref, fg_ref, sw_ref) = held
    (limits, sbuf, wbuf, s2, r2, xall, perm, hs, gs, r4, auxs, r5, ms, r6, fs, r7, load_sem, w_ssem, w_rsem, wc_ssem, wc_rsem, s2_ssem, s2_rsem, z_ssem, z_rsem, y_ssem, y_rsem, c_ssem, c_rsem, s4_ssem, s4_rsem, s5_ssem, s5_rsem, s6_ssem, s6_rsem, s7_ssem, s7_rsem) = refs
    dp = lax.axis_index("dp")
    b = lax.axis_index("blk")
    c = lax.rem(dp, 2)
    z = lax.rem(lax.div(dp, 2), nz)
    y = lax.div(dp, 2 * nz)
    yc = 2 * y + c
    conts = 4 * nz * CONT
    rows = 2 * nz

    def dev(y_, z_, c_, b_):
        return ((y_ * nz + z_) * 2 + c_, b_)

    def remote(src, dst, ssem, rsem, target):
        return pltpu.make_async_remote_copy(
            src_ref=src, dst_ref=dst, send_sem=ssem, recv_sem=rsem, device_id=target, device_id_type=MESH
        )

    barrier = pltpu.get_barrier_semaphore()

    def greet_plane(k, _):
        other = lax.rem(b * 4 + yc + k, 32)
        oyc, ob = lax.rem(other, 4), lax.div(other, 4)
        pl.semaphore_signal(
            barrier, inc=1, device_id=dev(lax.div(oyc, 2), z, lax.rem(oyc, 2), ob), device_id_type=MESH
        )
        return 0

    def greet_line(k, _):
        pl.semaphore_signal(barrier, inc=1, device_id=dev(y, lax.rem(z + k, nz), c, b), device_id_type=MESH)
        return 0

    loads = [pltpu.make_async_copy(sources[i], held[i], load_sem.at[i]) for i in range(16)]
    for load in loads:
        load.start()

    lax.fori_loop(1, 32, greet_plane, 0)
    lax.fori_loop(1, nz, greet_line, 0)

    for load in loads[2:8]:
        load.wait()

    wbuf[yc, b] = down_ref[...]
    me16 = y * NB + b

    def w_copy(k):
        other = lax.rem(me16 + k, 16)
        return remote(
            wbuf.at[yc, b],
            wbuf.at[yc, b],
            w_ssem.at[k],
            w_rsem.at[k],
            dev(lax.div(other, NB), z, c, lax.rem(other, NB)),
        )

    def wc_copy(i):
        return remote(
            wbuf.at[2 * i + c], wbuf.at[2 * i + c], wc_ssem.at[i], wc_rsem.at[i], dev(y, z, 1 - c, b)
        )

    r64, c64 = iota((64, 64), 0), iota((64, 64), 1)
    q_src = (r64 % 16) * 4 + ((r64 // 16) % 2) * 2 + r64 // 32
    q = dot(onehot(q_src == c64), q_ref[...]).astype(BF16)

    pl.semaphore_wait(barrier, 31 + nz - 1)
    lax.fori_loop(1, 16, lambda k, _: (w_copy(k).start(), 0)[1], 0)

    lane = iota((64, 256), 1)
    even = lane % 2 == 0
    tok = lane // 2
    page_no = iota((PAGES, PAGES), 0) == jnp.broadcast_to(tab_ref[...], (PAGES, PAGES))
    logical = jnp.sum(jnp.where(page_no, iota((PAGES, PAGES), 1), 0), -1, keepdims=True)
    limits[...] = jnp.broadcast_to(plen_ref[0] - logical * 128, (PAGES, 256))
    factor = 1.0 / math.sqrt(HD)

    def page_rows(l):
        return kv[pl.ds(pl.multiple_of(l * 256, 256), 256), :]

    loads[0].wait()

    def scores(i, best):
        for u in range(4):
            l = i * 4 + u
            s = dot_nt(q, page_rows(l))
            s = jnp.where(even & (tok < limits[pl.ds(l, 1), :]), s, NEG)
            sbuf[:, pl.ds(pl.multiple_of(l * 256, 256), 256)] = s
            best = jnp.maximum(best, s)
        return best

    best = lax.fori_loop(0, PAGES // 4, scores, jnp.full((64, 256), NEG, F32))
    loads[1].wait()
    owner = iota((64, 256), 0) % 16

    def tail_scores(i, s_tail):
        for u in range(4):
            t = i * 4 + u
            s = dot_nt(q, tail[pl.ds(pl.multiple_of(t * 256, 256), 256), :])
            s_tail = jnp.where((owner == t) & even & (tok < tlen_ref[0, t]), s, s_tail)
        return s_tail

    s_tail = lax.fori_loop(0, CONT // 4, tail_scores, jnp.full((64, 256), NEG, F32))
    new_cont, new_tok = c64 // 4, (c64 // 2) % 2
    new_ok = (c64 % 2 == 0) & (new_cont == r64 % 16) & (new_tok <= (r64 // 16) % 2)
    s_new = jnp.where(new_ok, dot_nt(q, new_ref[...]), NEG)
    top = jnp.maximum(
        jnp.max(jnp.maximum(best, s_tail), -1, keepdims=True), jnp.max(s_new, -1, keepdims=True)
    )
    w_tail = jnp.exp((s_tail - top) * factor)
    w_new = jnp.exp((s_new - top) * factor)
    v_tail = pltpu.roll(w_tail, 1, 1)
    mixed = dot(pltpu.roll(w_new, 1, 1).astype(BF16), new_ref[...])

    def values(i, state):
        total, acc = state
        for u in range(4):
            l = i * 4 + u
            w = jnp.exp((sbuf[:, pl.ds(pl.multiple_of(l * 256, 256), 256)] - top) * factor)
            total = total + w
            acc = acc + dot(pltpu.roll(w, 1, 1).astype(BF16), page_rows(l))
        return total, acc

    total, mixed = lax.fori_loop(0, PAGES // 4, values, (w_tail, mixed))

    def tail_values(i, acc):
        for u in range(4):
            t = i * 4 + u
            w = jnp.where(owner == t, v_tail, 0.0).astype(BF16)
            acc = acc + dot(w, tail[pl.ds(pl.multiple_of(t * 256, 256), 256), :])
        return acc

    mixed = lax.fori_loop(0, CONT // 4, tail_values, mixed)
    total = jnp.sum(total, -1, keepdims=True) + jnp.sum(w_new, -1, keepdims=True)
    attn = (mixed / total).astype(BF16)

    loads[8].wait()
    for i in range(NB):
        cols = slice(i * FB, (i + 1) * FB)
        s2[i] = (dot(attn[:32], ow[:HD, cols]) + dot(attn[32:], ow[HD:, cols])).astype(BF16)

    def s2_copy(k):
        other = lax.rem(b + k, NB)
        return remote(s2.at[other], r2.at[k - 1], s2_ssem.at[k], s2_rsem.at[k], dev(y, z, c, other))

    lax.fori_loop(1, NB, lambda k, _: (s2_copy(k).start(), 0)[1], 0)

    for load in loads[9:]:
        load.wait()
    mig = mig_ref[...]
    home = mig // CONT
    stored = ((home // (2 * nz) * 2 + home % 2) * nz + (home // 2) % nz) * CONT + mig % CONT
    chunk = 4 * rows
    lines = mig.shape[0]
    p_row = iota((chunk, 1), 0)
    first = ((p_row // (2 * rows)) * nz + (p_row // 2) % nz) * 32 + ((p_row // rows) % 2) * 16 + p_row % 2
    line = onehot(iota((chunk, lines), 1) == first // 128)
    spread_mig = dot(line, (stored // 32).astype(F32).astype(BF16)) * 32.0 + dot(
        line, (stored % 32).astype(F32).astype(BF16)
    )
    slot_lane = iota((chunk, 128), 1) - first % 128
    for i in range(NB):
        column = jnp.sum(jnp.where(slot_lane == 2 * i, spread_mig, 0.0), -1, keepdims=True)
        perm[i] = onehot(iota((chunk, conts), 1) == column.astype(jnp.int32))
    gains = gain_ref[...].astype(F32)
    g_row = iota((16, 128), 0)
    gain = jnp.concatenate(
        [
            jnp.sum(jnp.where(g_row == 2 * b, gains, 0.0), 0, keepdims=True),
            jnp.sum(jnp.where(g_row == 2 * b + 1, gains, 0.0), 0, keepdims=True),
        ],
        1,
    )
    gate_t = (gate_ref[...].astype(F32) * gain).astype(BF16)
    up_t = (up_ref[...].astype(F32) * gain).astype(BF16)
    none32 = jnp.zeros((32, FB), BF16)
    none96 = jnp.zeros((96, FB), BF16)
    w_first = jnp.concatenate([gate_t, none32, up_t, none32], 0)
    w_second = jnp.concatenate(
        [none96, gate_t[:32], none96, up_t[:32], gate_t[32:], up_t[32:]], 0
    )
    r32, c32 = iota((32, 32), 0), iota((32, 32), 1)
    order = onehot((r32 % 16) * 2 + r32 // 16 == c32)
    resid = dot(order, resid_ref[:, pl.ds(pl.multiple_of(b * FB, FB), FB)])

    sel_r, sel_c = iota((128, NB * rows), 0), iota((128, NB * rows), 1)
    place = sel_r % 16
    own_rows = jnp.concatenate([perm[i, pl.ds(pl.multiple_of(yc * rows, rows), rows), :] for i in range(NB)], 0)
    sel = [
        dot(
            onehot(
                (place < 4)
                & (place % 2 == n)
                & (sel_c == (sel_r // 16) * rows + z * 2 + (place // 2) % 2)
            ),
            own_rows,
        ).astype(BF16)
        for n in range(2)
    ]

    lax.fori_loop(1, NB, lambda k, _: (s2_copy(k).wait_recv(), 0)[1], 0)
    mid = resid + s2[b].astype(F32)
    for k in range(1, NB):
        mid = mid + r2[k - 1].astype(F32)
    xall[0, yc, z] = mid[:16].astype(BF16)
    xall[1, yc, z] = mid[16:].astype(BF16)

    def z_copy(source, step, slot):
        piece = xall.at[:, yc, source]
        return remote(piece, piece, z_ssem.at[slot], z_rsem.at[slot], dev(y, lax.rem(z + step + nz, nz), c, b))

    def y_copy(source, slot):
        piece = xall.at[:, yc, source]
        return remote(piece, piece, y_ssem.at[slot], y_rsem.at[slot], dev(1 - y, z, c, b))

    def c_copy(i):
        piece = xall.at[:, 2 * i + c]
        return remote(piece, piece, c_ssem.at[i], c_rsem.at[i], dev(y, z, 1 - c, b))

    far = {1: nz // 2, -1: (nz - 1) // 2}
    z_waits = []

    def z_forward(way, stage):
        source = lax.rem(z - way * stage * radix + nz, nz)
        for j in range(1, radix + 1):
            dist = stage * radix + j
            if dist <= far[way]:
                copy = z_copy(source, way * j, (way * dist) % nz)
                copy.start()
                z_waits.append(copy)

    def z_arrived(way, dist):
        slot = (way * dist) % nz
        z_copy(z, 0, slot).wait_recv()
        return lax.rem(z - way * dist + nz, nz)

    z_forward(1, 0)
    z_forward(-1, 0)
    y_waits = [y_copy(z, 0)]
    y_waits[0].start()
    for dist in range(1, nz // 2 + 1):
        for way in (1, -1):
            if dist <= far[way]:
                source = z_arrived(way, dist)
                if dist % radix == 0:
                    z_forward(way, dist // radix)
                copy = y_copy(source, (way * dist) % nz)
                copy.start()
                y_waits.append(copy)
    c_copy(y).start()
    for copy in y_waits:
        copy.wait_recv()
    c_copy(1 - y).start()

    lax.fori_loop(1, 16, lambda k, _: (w_copy(k).wait_recv(), 0)[1], 0)
    wc_copy(0).start()
    wc_copy(1).start()

    c_copy(0).wait_recv()
    c_copy(1).wait_recv()

    x0 = xall[0].reshape(conts, FB)
    x1 = xall[1].reshape(conts, FB)
    h1 = dot_nt(x1, w_second)
    hs[:, :256] = (dot_nt(x0, w_first) + h1[:, :256]).astype(BF16)
    hs[:, 256:384] = h1[:, 256:].astype(BF16)
    e_lane = iota((FB, 128), 1)
    sq0 = (x0.astype(F32) * x0.astype(F32)).astype(BF16)
    sq1 = (x1.astype(F32) * x1.astype(F32)).astype(BF16)
    squares = dot(sq0, onehot((e_lane == 0) | (e_lane == 2))) + dot(sq1, onehot((e_lane == 1) | (e_lane == 3)))
    high = squares.astype(BF16).astype(F32)
    hs[:, 384:] = jnp.where(iota((conts, 128), 1) < 2, high, squares - high).astype(BF16)

    res = dot(sel[0], x0) + dot(sel[1], x1)
    fg = fg_ref[...].astype(F32)
    sw = sw_ref[...].astype(F32)
    a_row = iota((128, FB), 0) % 16
    res = jnp.where(a_row == 4, jnp.concatenate([fg[0:1], fg[1:2]], 1), res)
    res = jnp.where(a_row == 5, jnp.concatenate([sw[0:1], sw[1:2]], 1), res).astype(BF16)
    for i in range(NB):
        auxs[i, rows : rows + 16, :] = res[i * 16 : (i + 1) * 16]

    def s4_copy(i, j):
        ob, oyc = lax.rem(b + i, NB), lax.rem(yc + j, 4)
        return remote(
            gs.at[ob, oyc],
            r4.at[yc, b],
            s4_ssem.at[i * 4 + j],
            s4_rsem.at[i * 4 + j],
            dev(lax.div(oyc, 2), z, lax.rem(oyc, 2), ob),
        )

    def s5_copy(i):
        ob = lax.rem(b + i, NB)
        return remote(auxs.at[ob], r5.at[b], s5_ssem.at[i], s5_rsem.at[i], dev(y, z, c, ob))

    def serve(i):
        ob = lax.rem(b + i, NB)
        g = dot(perm[ob], hs[...]).astype(BF16)
        gs[ob] = g[:, :384].reshape(4, rows, 384)
        return ob, g[:, 384:].reshape(4, rows, 128)

    def aux_rows(ob, squares4):
        pick = jnp.zeros((rows, 128), BF16)
        for i in range(4):
            pick = jnp.where(yc == i, squares4[i], pick)
        auxs[ob, :rows, :128] = pick
        auxs[ob, :rows, 128:] = jnp.zeros((rows, 128), BF16)

    def serve_send(i, _):
        ob, squares4 = serve(i)
        for j in range(4):
            s4_copy(i, j).start()
        aux_rows(ob, squares4)
        s5_copy(i).start()
        return 0

    lax.fori_loop(1, NB, serve_send, 0)
    ob, squares4 = serve(0)
    for j in range(1, 4):
        s4_copy(0, j).start()
    aux_rows(ob, squares4)
    r4[yc, b] = gs[b, yc]
    r5[b] = auxs[b]

    lax.fori_loop(1, NB, lambda k, _: (s5_copy(k).wait_recv(), 0)[1], 0)
    stats = r5[0, :rows, :128].astype(F32)
    for i in range(1, NB):
        stats = stats + r5[i, :rows, :128].astype(F32)
    l128 = iota((rows, 128), 1)

    def inverse_rms(n):
        picked = jnp.where(l128 % 2 == n, jnp.where(l128 < 4, stats, 0.0), 0.0)
        return lax.rsqrt(jnp.sum(picked, -1, keepdims=True) / D + EPS)

    scale0, scale1 = inverse_rms(0), inverse_rms(1)
    scale_ab = jnp.where(l128 < 96, scale0, scale1)

    lax.fori_loop(1, 32, lambda k, _: (s4_copy(lax.div(k, 4), lax.rem(k, 4)).wait_recv(), 0)[1], 0)

    def silu(v):
        return v / (1.0 + jnp.exp(-v))

    mr, mc = iota((nz * 16, 2 * rows), 0), iota((nz * 16, 2 * rows), 1)
    m_in = mr % 4
    m_src = (m_in % 2) * rows + (mr // 16) * 2 + m_in // 2
    spread = [onehot((mc == m_src) & ((mr // 4) % 4 == j)) for j in range(4)]

    def hidden(g):
        acc = r4[g, 0].astype(F32)
        for i in range(1, NB):
            acc = acc + r4[g, i].astype(F32)
        h_ab = silu(acc[:, :128] * scale_ab) * (acc[:, 128:256] * scale_ab)
        last = acc[:, 256:] * scale1
        h_c = silu(last) * pltpu.roll(last, 64, 1)
        h_one = jnp.where(l128 < 32, pltpu.roll(h_ab, 32, 1), pltpu.roll(h_c, 32, 1))
        return jnp.concatenate([h_ab, h_one], 0).astype(BF16)

    hids = [hidden(g) for g in range(4)]
    wc_copy(0).wait_recv()
    wc_copy(1).wait_recv()
    left = jnp.zeros((nz * 16, FB), F32)
    right = jnp.zeros((nz * 16, FB), F32)
    for g in range(4):
        for j in range(4):
            lhs = dot(spread[j], hids[g]).astype(BF16)[:, :HOLD]
            left = left + dot(lhs, wbuf[g, 2 * j])
            right = right + dot(lhs, wbuf[g, 2 * j + 1])
    ms[:, :, :FB] = left.astype(BF16).reshape(nz, 16, FB)
    ms[:, :, FB:] = right.astype(BF16).reshape(nz, 16, FB)

    def s6_copy(k):
        other = lax.rem(z + k, nz)
        return remote(ms.at[other], r6.at[z], s6_ssem.at[k], s6_rsem.at[k], dev(y, other, c, b))

    lax.fori_loop(1, nz, lambda k, _: (s6_copy(k).start(), 0)[1], 0)
    r6[z] = ms[z]

    def gathered(pick):
        return jnp.concatenate(
            [jnp.concatenate([pick(2 * j), pick(2 * j + 1)], 1) for j in range(4)], 0
        )

    resid4 = gathered(lambda i: r5[i, rows : rows + 16, :].astype(F32)[0:4])
    weight4 = gathered(
        lambda i: jnp.broadcast_to(
            r5[i, rows : rows + 16, :].astype(F32)[4:5] * r5[i, rows : rows + 16, :].astype(F32)[5:6], (4, FB)
        )
    )

    lax.fori_loop(1, nz, lambda k, _: (s6_copy(k).wait_recv(), 0)[1], 0)
    moved = resid4
    for k in range(nz):
        moved = moved + r6[k].astype(F32)
    ss = jnp.sum(moved * moved, -1, keepdims=True)
    st = jnp.sum(moved * weight4, -1, keepdims=True)
    ss = ss[0:4] + ss[4:8] + ss[8:12] + ss[12:16]
    st = st[0:4] + st[4:8] + st[8:12] + st[12:16]
    score = jnp.broadcast_to(st * lax.rsqrt(ss / D + EPS), (4, FB))
    for i in range(NB):
        j, half = i // 2, i % 2
        fs[i] = jnp.concatenate([moved[4 * j : 4 * j + 4, half * FB : (half + 1) * FB], score], 0)

    def s7_copy(k):
        other = lax.rem(b + k, NB)
        return remote(fs.at[other], r7.at[b], s7_ssem.at[k], s7_rsem.at[k], dev(y, z, c, other))

    lax.fori_loop(1, NB, lambda k, _: (s7_copy(k).start(), 0)[1], 0)
    r7[b] = fs[b]

    lax.fori_loop(1, 16, lambda k, _: (w_copy(k).wait_send(), 0)[1], 0)
    wc_copy(0).wait_send()
    wc_copy(1).wait_send()
    lax.fori_loop(1, NB, lambda k, _: (s2_copy(k).wait_send(), 0)[1], 0)
    for copy in z_waits + y_waits:
        copy.wait_send()
    c_copy(0).wait_send()
    c_copy(1).wait_send()
    lax.fori_loop(1, 32, lambda k, _: (s4_copy(lax.div(k, 4), lax.rem(k, 4)).wait_send(), 0)[1], 0)
    lax.fori_loop(1, NB, lambda k, _: (s5_copy(k).wait_send(), 0)[1], 0)
    lax.fori_loop(1, nz, lambda k, _: (s6_copy(k).wait_send(), 0)[1], 0)

    lax.fori_loop(1, NB, lambda k, _: (s7_copy(k).wait_recv(), 0)[1], 0)
    final = jnp.concatenate([r7[i][:4] for i in range(NB)], 0)
    out_ref[...] = final.astype(BF16)
    col = jnp.concatenate([r7[i][4:, :32] for i in range(NB)], 0)
    score_ref[...] = jnp.sum(jnp.where(r32 == c32, col, 0.0), 0, keepdims=True)
    lax.fori_loop(1, NB, lambda k, _: (s7_copy(k).wait_send(), 0)[1], 0)


def shards(
    nz,
    resid,
    queries,
    new_kv,
    prefix_pool,
    page_table,
    prompt_len,
    tail_pool,
    tail_len,
    migration,
    out_w,
    mlp_gain,
    gate_w,
    up_w,
    down_w,
    final_gain,
    score_w,
):
    conts = 4 * nz * CONT
    rows = 2 * nz
    vmem = pl.BlockSpec(memory_space=pltpu.VMEM)
    hbm = pl.BlockSpec(memory_space=pl.ANY)
    dma = pltpu.SemaphoreType.DMA
    out, score = pl.pallas_call(
        functools.partial(kernel, nz, 4),
        out_shape=(
            jax.ShapeDtypeStruct((32, FB), BF16),
            jax.ShapeDtypeStruct((1, 32), F32),
        ),
        in_specs=[hbm] * 16,
        out_specs=(vmem, vmem),
        scratch_shapes=[
            pltpu.VMEM((PAGES * 256, HD), BF16),
            pltpu.VMEM((CONT * 256, HD), BF16),
            pltpu.VMEM((64, HD), BF16),
            pltpu.VMEM((64, HD), BF16),
            pltpu.VMEM((1, PAGES), jnp.int32),
            pltpu.SMEM((1,), jnp.int32),
            pltpu.SMEM((1, CONT), jnp.int32),
            pltpu.VMEM((HOLD, FB), BF16),
            pltpu.VMEM((2 * HD, D), BF16),
            pltpu.VMEM((32, D), BF16),
            pltpu.VMEM((conts // 128, 128), jnp.int32),
            pltpu.VMEM((HOLD, FB), BF16),
            pltpu.VMEM((HOLD, FB), BF16),
            pltpu.VMEM((16, 128), BF16),
            pltpu.VMEM((2, 128), BF16),
            pltpu.VMEM((2, 128), BF16),
            pltpu.VMEM((PAGES, 256), jnp.int32),
            pltpu.VMEM((64, PAGES * 256), F32),
            pltpu.VMEM((4, NB, HOLD, FB), BF16),
            pltpu.VMEM((NB, 32, FB), BF16),
            pltpu.VMEM((NB - 1, 32, FB), BF16),
            pltpu.VMEM((2, 4, nz, CONT, FB), BF16),
            pltpu.VMEM((NB, 4 * rows, conts), BF16),
            pltpu.VMEM((conts, 512), BF16),
            pltpu.VMEM((NB, 4, rows, 384), BF16),
            pltpu.VMEM((4, NB, rows, 384), BF16),
            pltpu.VMEM((NB, rows + 16, FB), BF16),
            pltpu.VMEM((NB, rows + 16, FB), BF16),
            pltpu.VMEM((nz, 16, 512), BF16),
            pltpu.VMEM((nz, 16, 512), BF16),
            pltpu.VMEM((NB, 8, FB), F32),
            pltpu.VMEM((NB, 8, FB), F32),
            dma((16,)),
            dma((16,)),
            dma((16,)),
            dma((2,)),
            dma((2,)),
            dma((NB,)),
            dma((NB,)),
            dma((nz,)),
            dma((nz,)),
            dma((nz,)),
            dma((nz,)),
            dma((2,)),
            dma((2,)),
            dma((32,)),
            dma((32,)),
            dma((NB,)),
            dma((NB,)),
            dma((nz,)),
            dma((nz,)),
            dma((NB,)),
            dma((NB,)),
        ],
        compiler_params=pltpu.CompilerParams(
            collective_id=0, has_side_effects=True, vmem_limit_bytes=58 * 1024 * 1024
        ),
    )(
        prefix_pool.reshape(PAGES * 256, HD),
        tail_pool.reshape(CONT * 256, HD),
        queries.reshape(64, HD),
        new_kv.reshape(64, HD),
        page_table,
        prompt_len,
        tail_len,
        down_w,
        out_w,
        resid,
        migration.reshape(conts // 128, 128),
        gate_w.T,
        up_w.T,
        mlp_gain.reshape(16, 128),
        final_gain.reshape(2, 128),
        score_w.reshape(2, 128),
    )
    return out, score.reshape(32)


def solution(mesh):
    nz = mesh.shape["dp"] // 4
    return jax.shard_map(
        functools.partial(shards, nz),
        mesh=mesh,
        in_specs=(
            P("dp", None),
            P("dp", "blk", None),
            P("dp", None, "blk", None),
            P("dp", None, None, "blk", None),
            P("dp", None),
            P("dp"),
            P("dp", None, None, "blk", None),
            P("dp", None),
            P(),
            P("blk", None),
            P(),
            P("blk", "dp"),
            P("blk", "dp"),
            P("dp", "blk"),
            P("blk"),
            P("blk"),
        ),
        out_specs=(P("dp", "blk"), P("dp")),
        check_vma=False,
    )
```

time: 632 us -> 97 us (0.15)
  waiting for transfers between devices: 537 us -> 0 us
  Pallas kernels: 0 us -> 92.3 us
  local copies, waits for them, and re-layouts: 31.4 us -> 2.46 us
  blocking collectives: 22.2 us -> 0 us
  matrix products: 14.3 us -> 0 us
  between operations: 14.7 us -> 1.29 us
  other arithmetic: 10.8 us -> 0 us
    reduce_scatter x1 -> x0, waiting for transfers between devices: 227 us -> none  [shards(): lax.psum_scatter(term + jnp.where(own_rows[:, None], carried, 0.0), 'dp',...]
    psum x2 -> x0, waiting for transfers between devices: 190 us -> none  [the longest x1 101 us: shards(): lax.psum(partial_value.astype(jnp.bfloat16), 'blk').astype(jnp.float32)]
    all_gather x1 -> x0, waiting for transfers between devices: 120 us -> none  [shards(): piece = lax.all_gather(feat_slice, 'dp', axis=0, tiled=True)]
    pallas_call x0 -> x1, Pallas kernels: none -> 92.3 us  [shards(): pl.pallas_call(functools.partial(kernel, nz, 4), out_shape=(jax.ShapeDtyp...]
    gather x4 -> x0, local copies, waits for them, and re-layouts: 24.5 us -> none  [the longest x2 9.73 us: attend_prompt(): prefix = jnp.take(pool, table, axis=0).reshape(-1, 2, groups, width)]
    psum x1 -> x0, blocking collectives: 22.2 us -> none  [shards(): lax.psum((jnp.sum(moved * moved, -1), jnp.sum(moved * weighted, -1)), 'blk')]
    dot_general x10 -> x0, matrix products: 14.3 us -> none  [the longest x1 4.85 us: shards(): jnp.dot(jnp.take(hidden, source, axis=0), down_w, preferred_element_type=...]
  transfers between devices with their start and end apart: 4 -> 0, of which waited for: 4 -> 0; matrix products, arithmetic and copies ran while one was open for 2% -> 0% of each run, Pallas kernels for 0% -> 0%
where the time goes in v1:
time: 97 us; the launch traced here: 96.1 us
  Pallas kernels  92.3 us (95%)
  local copies, waits for them, and re-layouts  2.46 us (3%)
  between operations  1.29 us (1%)
    pallas_call x1, Pallas kernels, shards(): pl.pallas_call(functools.partial(kernel, nz, 4), out_shape=(jax.ShapeDtyp...  92.3 us
    unnamed x2, local copies, waits for them, and re-layouts  2.46 us

profile of v1, /device:TPU:24, one launch (start us, length us, event | category | flops | bytes accessed | tf_op | source)
XLA Modules:
  0.0 96.1 jit_solution(204640612880951192)
XLA Ops:
  1.3 92.3 %shard_map.167 = (bf16[32,256]{1,0:T(8,128)(2,1)}, f32[1,32]{1,0:T(1,128)}) custom-call(bf16[8192,128]{1,0:T(8,128)(2,1)} %bitcast.11, bf16[4096,128]{1,0:T(8,128)(2,1)} %bitcast.12, bf16[64,128]{1,0:T(8,128)(2,1)} %bitcast.15, bf16[64,128]{1,0:T(8,128)(2,1)} %bitcast.16, s32[1,32]{1,0:T(1,128)} %refs_4_.1, s32[1]{0:T(128)S(6)} %copy.20.refs_5_, ...), custom_call_target="tpu_custom_call" | custom-call | tf_op jit(solution)/shard_map/pallas_call | solution.py:500
  93.6 1.3 %copy.21 = bf16[32,256]{1,0:T(8,128)(2,1)} copy(bf16[32,256]{1,0:T(8,128)(2,1)} %get-tuple-element.8) | data formatting | bytes 32768
  94.9 1.1 %copy.22 = f32[32]{0:T(128)} copy(f32[32]{0:T(128)} %bitcast.21) | data formatting | bytes 256

commit v2 on v1

--- a/solution.py
+++ b/solution.py
@@ -20,6 +20,7 @@
 CONT = 16
 PAGES = 32
 HD = 128
+TREE = ((0, (5, 2, 1)), (2, (4, 3)), (5, (8, 7, 6)))
 
 
 def iota(shape, dim):
@@ -40,12 +41,11 @@
 
 def kernel(
     nz,
-    radix,
     *refs,
 ):
-    sources, (out_ref, score_ref), held, refs = refs[:16], refs[16:18], refs[18:34], refs[34:]
+    sources, out_ref, held, refs = refs[:16], refs[16], refs[17:33], refs[33:]
     (kv, tail, q_ref, new_ref, tab_ref, plen_ref, tlen_ref, down_ref, ow, resid_ref, mig_ref, gate_ref, up_ref, gain_ref, fg_ref, sw_ref) = held
-    (limits, sbuf, wbuf, s2, r2, xall, perm, hs, gs, r4, auxs, r5, ms, r6, fs, r7, load_sem, w_ssem, w_rsem, wc_ssem, wc_rsem, s2_ssem, s2_rsem, z_ssem, z_rsem, y_ssem, y_rsem, c_ssem, c_rsem, s4_ssem, s4_rsem, s5_ssem, s5_rsem, s6_ssem, s6_rsem, s7_ssem, s7_rsem) = refs
+    (bias, sbuf, wbuf, s2, r2, xall, perm, sel, hs, gs, r4, auxs, r5, ms, ags, r6, fs, r7, load_sem, w_ssem, w_rsem, wc_ssem, wc_rsem, s2_ssem, s2_rsem, z_ssem, z_rsem, y_ssem, y_rsem, c_ssem, c_rsem, s4_ssem, s4_rsem, s5_ssem, s5_rsem, s6_ssem, s6_rsem, s7_ssem, s7_rsem) = refs
     dp = lax.axis_index("dp")
     b = lax.axis_index("blk")
     c = lax.rem(dp, 2)
@@ -109,73 +109,67 @@
     q_src = (r64 % 16) * 4 + ((r64 // 16) % 2) * 2 + r64 // 32
     q = dot(onehot(q_src == c64), q_ref[...]).astype(BF16)
 
+    lane = iota((PAGES, 256), 1)
+    page_no = iota((PAGES, PAGES), 0) == jnp.broadcast_to(tab_ref[...], (PAGES, PAGES))
+    logical = jnp.sum(jnp.where(page_no, iota((PAGES, PAGES), 1), 0), -1, keepdims=True)
+    limit = jnp.broadcast_to(plen_ref[0] - logical * 128, (PAGES, 256))
+    bias[...] = jnp.where((lane % 2 == 0) & (lane // 2 < limit), 0.0, NEG)
+    unit = math.log2(math.e) / math.sqrt(HD)
+
+    def widest(best, s):
+        for i in range(s.shape[1] // 128):
+            best = jnp.maximum(best, s[:, i * 128 : (i + 1) * 128])
+        return best
+
+    def next_lane(w):
+        return jnp.concatenate(
+            [pltpu.roll(w[:, i * 128 : (i + 1) * 128], 1, 1) for i in range(w.shape[1] // 128)], 1
+        ).astype(BF16)
+
+    loads[0].wait()
+    best = jnp.full((64, 128), NEG, F32)
+    for i in range(PAGES // 8):
+        s = dot_nt(q, kv[i * 2048 : (i + 1) * 2048, :])
+        for u in range(8):
+            l = i * 8 + u
+            part = s[:, u * 256 : (u + 1) * 256] + bias[l : l + 1, :]
+            sbuf[:, l * 256 : (l + 1) * 256] = part
+            best = widest(best, part)
+    loads[1].wait()
+    owner = iota((64, 256), 0) % 16
+    t_lane = iota((1, 256), 1)
+    s_tail = jnp.full((64, 256), NEG, F32)
+    for i in range(CONT // 8):
+        s = dot_nt(q, tail[i * 2048 : (i + 1) * 2048, :])
+        for u in range(8):
+            t = i * 8 + u
+            t_bias = jnp.where((t_lane % 2 == 0) & (t_lane // 2 < tlen_ref[0, t]), 0.0, NEG)
+            s_tail = jnp.where(owner == t, s[:, u * 256 : (u + 1) * 256] + t_bias, s_tail)
+
     pl.semaphore_wait(barrier, 31 + nz - 1)
     lax.fori_loop(1, 16, lambda k, _: (w_copy(k).start(), 0)[1], 0)
 
-    lane = iota((64, 256), 1)
-    even = lane % 2 == 0
-    tok = lane // 2
-    page_no = iota((PAGES, PAGES), 0) == jnp.broadcast_to(tab_ref[...], (PAGES, PAGES))
-    logical = jnp.sum(jnp.where(page_no, iota((PAGES, PAGES), 1), 0), -1, keepdims=True)
-    limits[...] = jnp.broadcast_to(plen_ref[0] - logical * 128, (PAGES, 256))
-    factor = 1.0 / math.sqrt(HD)
-
-    def page_rows(l):
-        return kv[pl.ds(pl.multiple_of(l * 256, 256), 256), :]
-
-    loads[0].wait()
-
-    def scores(i, best):
-        for u in range(4):
-            l = i * 4 + u
-            s = dot_nt(q, page_rows(l))
-            s = jnp.where(even & (tok < limits[pl.ds(l, 1), :]), s, NEG)
-            sbuf[:, pl.ds(pl.multiple_of(l * 256, 256), 256)] = s
-            best = jnp.maximum(best, s)
-        return best
-
-    best = lax.fori_loop(0, PAGES // 4, scores, jnp.full((64, 256), NEG, F32))
-    loads[1].wait()
-    owner = iota((64, 256), 0) % 16
-
-    def tail_scores(i, s_tail):
-        for u in range(4):
-            t = i * 4 + u
-            s = dot_nt(q, tail[pl.ds(pl.multiple_of(t * 256, 256), 256), :])
-            s_tail = jnp.where((owner == t) & even & (tok < tlen_ref[0, t]), s, s_tail)
-        return s_tail
-
-    s_tail = lax.fori_loop(0, CONT // 4, tail_scores, jnp.full((64, 256), NEG, F32))
     new_cont, new_tok = c64 // 4, (c64 // 2) % 2
     new_ok = (c64 % 2 == 0) & (new_cont == r64 % 16) & (new_tok <= (r64 // 16) % 2)
     s_new = jnp.where(new_ok, dot_nt(q, new_ref[...]), NEG)
     top = jnp.maximum(
-        jnp.max(jnp.maximum(best, s_tail), -1, keepdims=True), jnp.max(s_new, -1, keepdims=True)
+        jnp.max(widest(best, s_tail), -1, keepdims=True), jnp.max(s_new, -1, keepdims=True)
     )
-    w_tail = jnp.exp((s_tail - top) * factor)
-    w_new = jnp.exp((s_new - top) * factor)
-    v_tail = pltpu.roll(w_tail, 1, 1)
+    w_tail = jnp.exp2((s_tail - top) * unit)
+    w_new = jnp.exp2((s_new - top) * unit)
+    total = w_tail[:, :128] + w_tail[:, 128:]
     mixed = dot(pltpu.roll(w_new, 1, 1).astype(BF16), new_ref[...])
-
-    def values(i, state):
-        total, acc = state
-        for u in range(4):
-            l = i * 4 + u
-            w = jnp.exp((sbuf[:, pl.ds(pl.multiple_of(l * 256, 256), 256)] - top) * factor)
-            total = total + w
-            acc = acc + dot(pltpu.roll(w, 1, 1).astype(BF16), page_rows(l))
-        return total, acc
-
-    total, mixed = lax.fori_loop(0, PAGES // 4, values, (w_tail, mixed))
-
-    def tail_values(i, acc):
-        for u in range(4):
-            t = i * 4 + u
-            w = jnp.where(owner == t, v_tail, 0.0).astype(BF16)
-            acc = acc + dot(w, tail[pl.ds(pl.multiple_of(t * 256, 256), 256), :])
-        return acc
-
-    mixed = lax.fori_loop(0, CONT // 4, tail_values, mixed)
+    for i in range(PAGES // 8):
+        w = jnp.exp2((sbuf[:, i * 2048 : (i + 1) * 2048] - top) * unit)
+        for u in range(16):
+            total = total + w[:, u * 128 : (u + 1) * 128]
+        mixed = mixed + dot(next_lane(w), kv[i * 2048 : (i + 1) * 2048, :])
+    v_tail = next_lane(w_tail)
+    for i in range(CONT // 8):
+        w = jnp.concatenate(
+            [jnp.where(owner == i * 8 + u, v_tail, jnp.zeros_like(v_tail)) for u in range(8)], 1
+        )
+        mixed = mixed + dot(w, tail[i * 2048 : (i + 1) * 2048, :])
     total = jnp.sum(total, -1, keepdims=True) + jnp.sum(w_new, -1, keepdims=True)
     attn = (mixed / total).astype(BF16)
 
@@ -231,8 +225,8 @@
     sel_r, sel_c = iota((128, NB * rows), 0), iota((128, NB * rows), 1)
     place = sel_r % 16
     own_rows = jnp.concatenate([perm[i, pl.ds(pl.multiple_of(yc * rows, rows), rows), :] for i in range(NB)], 0)
-    sel = [
-        dot(
+    for n in range(2):
+        picked = dot(
             onehot(
                 (place < 4)
                 & (place % 2 == n)
@@ -240,8 +234,8 @@
             ),
             own_rows,
         ).astype(BF16)
-        for n in range(2)
-    ]
+        for i in range(4):
+            sel[n, i] = picked[:, i * nz * CONT : (i + 1) * nz * CONT]
 
     lax.fori_loop(1, NB, lambda k, _: (s2_copy(k).wait_recv(), 0)[1], 0)
     mid = resid + s2[b].astype(F32)
@@ -263,60 +257,67 @@
         return remote(piece, piece, c_ssem.at[i], c_rsem.at[i], dev(y, z, 1 - c, b))
 
     far = {1: nz // 2, -1: (nz - 1) // 2}
-    z_waits = []
-
-    def z_forward(way, stage):
-        source = lax.rem(z - way * stage * radix + nz, nz)
-        for j in range(1, radix + 1):
-            dist = stage * radix + j
-            if dist <= far[way]:
-                copy = z_copy(source, way * j, (way * dist) % nz)
+    z_waits, y_waits = [], []
+
+    def z_forward(way, parent, kids):
+        source = lax.rem(z - way * parent + nz, nz)
+        for kid in kids:
+            if kid <= far[way]:
+                copy = z_copy(source, way * (kid - parent), (way * kid) % nz)
                 copy.start()
                 z_waits.append(copy)
 
-    def z_arrived(way, dist):
+    def y_forward(way, dist):
         slot = (way * dist) % nz
-        z_copy(z, 0, slot).wait_recv()
-        return lax.rem(z - way * dist + nz, nz)
-
-    z_forward(1, 0)
-    z_forward(-1, 0)
-    y_waits = [y_copy(z, 0)]
-    y_waits[0].start()
-    for dist in range(1, nz // 2 + 1):
+        copy = y_copy(lax.rem(z - way * dist + nz, nz), slot)
+        copy.start()
+        y_waits.append(copy)
+
+    for way in (1, -1):
+        z_forward(way, *TREE[0])
+    y_forward(1, 0)
+    kids_of = dict(TREE)
+    for dist in (2, 5, 1, 4, 3, 6, 7, 8):
         for way in (1, -1):
             if dist <= far[way]:
-                source = z_arrived(way, dist)
-                if dist % radix == 0:
-                    z_forward(way, dist // radix)
-                copy = y_copy(source, (way * dist) % nz)
-                copy.start()
-                y_waits.append(copy)
+                z_copy(z, 0, (way * dist) % nz).wait_recv()
+                if dist in kids_of:
+                    z_forward(way, dist, kids_of[dist])
+                y_forward(way, dist)
+
+    e_lane = iota((FB, 128), 1)
+    e_first = onehot((e_lane == 0) | (e_lane == 2))
+    e_second = onehot((e_lane == 1) | (e_lane == 3))
+
+    def project(block, res):
+        x0 = xall[0, block].reshape(nz * CONT, FB)
+        x1 = xall[1, block].reshape(nz * CONT, FB)
+        h1 = dot_nt(x1, w_second)
+        hs[block, :, :256] = (dot_nt(x0, w_first) + h1[:, :256]).astype(BF16)
+        hs[block, :, 256:384] = h1[:, 256:].astype(BF16)
+        sq0 = (x0.astype(F32) * x0.astype(F32)).astype(BF16)
+        sq1 = (x1.astype(F32) * x1.astype(F32)).astype(BF16)
+        squares = dot(sq0, e_first) + dot(sq1, e_second)
+        high = squares.astype(BF16).astype(F32)
+        hs[block, :, 384:] = jnp.where(iota((nz * CONT, 128), 1) < 2, high, squares - high).astype(BF16)
+        return res + dot(sel[0, block], x0) + dot(sel[1, block], x1)
+
     c_copy(y).start()
+    res = project(yc, jnp.zeros((128, FB), F32))
+    c_copy(y).wait_recv()
+    res = project(2 * y + 1 - c, res)
     for copy in y_waits:
         copy.wait_recv()
     c_copy(1 - y).start()
+    res = project(2 * (1 - y) + c, res)
 
     lax.fori_loop(1, 16, lambda k, _: (w_copy(k).wait_recv(), 0)[1], 0)
     wc_copy(0).start()
     wc_copy(1).start()
 
-    c_copy(0).wait_recv()
-    c_copy(1).wait_recv()
-
-    x0 = xall[0].reshape(conts, FB)
-    x1 = xall[1].reshape(conts, FB)
-    h1 = dot_nt(x1, w_second)
-    hs[:, :256] = (dot_nt(x0, w_first) + h1[:, :256]).astype(BF16)
-    hs[:, 256:384] = h1[:, 256:].astype(BF16)
-    e_lane = iota((FB, 128), 1)
-    sq0 = (x0.astype(F32) * x0.astype(F32)).astype(BF16)
-    sq1 = (x1.astype(F32) * x1.astype(F32)).astype(BF16)
-    squares = dot(sq0, onehot((e_lane == 0) | (e_lane == 2))) + dot(sq1, onehot((e_lane == 1) | (e_lane == 3)))
-    high = squares.astype(BF16).astype(F32)
-    hs[:, 384:] = jnp.where(iota((conts, 128), 1) < 2, high, squares - high).astype(BF16)
-
-    res = dot(sel[0], x0) + dot(sel[1], x1)
+    c_copy(1 - y).wait_recv()
+    res = project(2 * (1 - y) + 1 - c, res)
+
     fg = fg_ref[...].astype(F32)
     sw = sw_ref[...].astype(F32)
     a_row = iota((128, FB), 0) % 16
@@ -341,7 +342,7 @@
 
     def serve(i):
         ob = lax.rem(b + i, NB)
-        g = dot(perm[ob], hs[...]).astype(BF16)
+        g = dot(perm[ob], hs[...].reshape(conts, 512)).astype(BF16)
         gs[ob] = g[:, :384].reshape(4, rows, 384)
         return ob, g[:, 384:].reshape(4, rows, 128)
 
@@ -414,12 +415,21 @@
     ms[:, :, :FB] = left.astype(BF16).reshape(nz, 16, FB)
     ms[:, :, FB:] = right.astype(BF16).reshape(nz, 16, FB)
 
-    def s6_copy(k):
-        other = lax.rem(z + k, nz)
-        return remote(ms.at[other], r6.at[z], s6_ssem.at[k], s6_rsem.at[k], dev(y, other, c, b))
-
-    lax.fori_loop(1, nz, lambda k, _: (s6_copy(k).start(), 0)[1], 0)
-    r6[z] = ms[z]
+    def s6_copy(src, step, slot):
+        return remote(src, r6.at[slot], s6_ssem.at[slot], s6_rsem.at[slot], dev(y, lax.rem(z + step + nz, nz), c, b))
+
+    s6_waits = []
+
+    def s6_send(way, dist, step, src):
+        copy = s6_copy(src, way * step, (way * dist) % nz)
+        copy.start()
+        s6_waits.append(copy)
+
+    for parent, kids in reversed(TREE):
+        for kid in kids:
+            for way in (1, -1):
+                if kid <= far[way] and kid not in kids_of:
+                    s6_send(way, kid, kid - parent, ms.at[lax.rem(z + way * kid + nz, nz)])
 
     def gathered(pick):
         return jnp.concatenate(
@@ -433,10 +443,22 @@
         )
     )
 
-    lax.fori_loop(1, nz, lambda k, _: (s6_copy(k).wait_recv(), 0)[1], 0)
-    moved = resid4
-    for k in range(nz):
-        moved = moved + r6[k].astype(F32)
+    def s6_sum(way, kids, acc):
+        for kid in kids:
+            if kid <= far[way]:
+                slot = (way * kid) % nz
+                s6_copy(ms.at[z], 0, slot).wait_recv()
+                acc = acc + r6[slot].astype(F32)
+        return acc
+
+    for at, (parent, kids) in reversed(list(enumerate(TREE[1:]))):
+        for way in (1, -1):
+            if parent <= far[way]:
+                share = ms[lax.rem(z + way * parent + nz, nz)].astype(F32)
+                ags[(1 - way) // 2, at] = s6_sum(way, kids, share).astype(BF16)
+                s6_send(way, parent, parent, ags.at[(1 - way) // 2, at])
+    moved = resid4 + ms[z].astype(F32)
+    moved = s6_sum(-1, TREE[0][1][::-1], s6_sum(1, TREE[0][1][::-1], moved))
     ss = jnp.sum(moved * moved, -1, keepdims=True)
     st = jnp.sum(moved * weight4, -1, keepdims=True)
     ss = ss[0:4] + ss[4:8] + ss[8:12] + ss[12:16]
@@ -463,14 +485,18 @@
     c_copy(1).wait_send()
     lax.fori_loop(1, 32, lambda k, _: (s4_copy(lax.div(k, 4), lax.rem(k, 4)).wait_send(), 0)[1], 0)
     lax.fori_loop(1, NB, lambda k, _: (s5_copy(k).wait_send(), 0)[1], 0)
-    lax.fori_loop(1, nz, lambda k, _: (s6_copy(k).wait_send(), 0)[1], 0)
+    for copy in s6_waits:
+        copy.wait_send()
 
     lax.fori_loop(1, NB, lambda k, _: (s7_copy(k).wait_recv(), 0)[1], 0)
-    final = jnp.concatenate([r7[i][:4] for i in range(NB)], 0)
-    out_ref[...] = final.astype(BF16)
-    col = jnp.concatenate([r7[i][4:, :32] for i in range(NB)], 0)
-    score_ref[...] = jnp.sum(jnp.where(r32 == c32, col, 0.0), 0, keepdims=True)
+    out_ref[...] = r7[...]
     lax.fori_loop(1, NB, lambda k, _: (s7_copy(k).wait_send(), 0)[1], 0)
+
+
+def finish(parts_ref, out_ref, score_ref):
+    out_ref[...] = jnp.concatenate([parts_ref[i, :4, :] for i in range(NB)], 0).astype(BF16)
+    col = jnp.concatenate([parts_ref[i, 4:, :32] for i in range(NB)], 0)
+    score_ref[...] = jnp.sum(jnp.where(iota((32, 32), 0) == iota((32, 32), 1), col, 0.0), 0, keepdims=True)
 
 
 def shards(
@@ -497,14 +523,11 @@
     vmem = pl.BlockSpec(memory_space=pltpu.VMEM)
     hbm = pl.BlockSpec(memory_space=pl.ANY)
     dma = pltpu.SemaphoreType.DMA
-    out, score = pl.pallas_call(
-        functools.partial(kernel, nz, 4),
-        out_shape=(
-            jax.ShapeDtypeStruct((32, FB), BF16),
-            jax.ShapeDtypeStruct((1, 32), F32),
-        ),
+    parts = pl.pallas_call(
+        functools.partial(kernel, nz),
+        out_shape=jax.ShapeDtypeStruct((NB, 8, FB), F32),
         in_specs=[hbm] * 16,
-        out_specs=(vmem, vmem),
+        out_specs=vmem,
         scratch_shapes=[
             pltpu.VMEM((PAGES * 256, HD), BF16),
             pltpu.VMEM((CONT * 256, HD), BF16),
@@ -522,19 +545,21 @@
             pltpu.VMEM((16, 128), BF16),
             pltpu.VMEM((2, 128), BF16),
             pltpu.VMEM((2, 128), BF16),
-            pltpu.VMEM((PAGES, 256), jnp.int32),
+            pltpu.VMEM((PAGES, 256), F32),
             pltpu.VMEM((64, PAGES * 256), F32),
             pltpu.VMEM((4, NB, HOLD, FB), BF16),
             pltpu.VMEM((NB, 32, FB), BF16),
             pltpu.VMEM((NB - 1, 32, FB), BF16),
             pltpu.VMEM((2, 4, nz, CONT, FB), BF16),
             pltpu.VMEM((NB, 4 * rows, conts), BF16),
-            pltpu.VMEM((conts, 512), BF16),
+            pltpu.VMEM((2, 4, 128, nz * CONT), BF16),
+            pltpu.VMEM((4, nz * CONT, 512), BF16),
             pltpu.VMEM((NB, 4, rows, 384), BF16),
             pltpu.VMEM((4, NB, rows, 384), BF16),
             pltpu.VMEM((NB, rows + 16, FB), BF16),
             pltpu.VMEM((NB, rows + 16, FB), BF16),
             pltpu.VMEM((nz, 16, 512), BF16),
+            pltpu.VMEM((2, len(TREE) - 1, 16, 512), BF16),
             pltpu.VMEM((nz, 16, 512), BF16),
             pltpu.VMEM((NB, 8, FB), F32),
             pltpu.VMEM((NB, 8, FB), F32),
@@ -581,6 +606,15 @@
         final_gain.reshape(2, 128),
         score_w.reshape(2, 128),
     )
+    out, score = pl.pallas_call(
+        finish,
+        out_shape=(
+            jax.ShapeDtypeStruct((32, FB), BF16),
+            jax.ShapeDtypeStruct((1, 32), F32),
+        ),
+        in_specs=[vmem],
+        out_specs=(vmem, vmem),
+    )(parts)
     return out, score.reshape(32)
 
 

time: 97 us -> 86.4 us (0.89)
  the two profiles are of different devices: /device:TPU:24 before, /device:TPU:2 now
where the time goes in v2:
time: 86.4 us; the launch traced here: 86.2 us
  Pallas kernels  84.9 us (98%)
  between operations  1.29 us (1%)
    pallas_call x1, Pallas kernels, shards(): pl.pallas_call(functools.partial(kernel, nz), out_shape=jax.ShapeDtypeStr...  83.4 us

profile of v2, /device:TPU:2, one launch (start us, length us, event | category | flops | bytes accessed | tf_op | source)
XLA Modules:
  0.0 86.2 jit_solution(2734865404129681177)
XLA Ops:
  1.3 83.4 %shard_map.167.parts_ref = f32[8,8,256]{2,1,0:T(8,128)} custom-call(bf16[8192,128]{1,0:T(8,128)(2,1)} %bitcast.11, bf16[4096,128]{1,0:T(8,128)(2,1)} %bitcast.12, bf16[64,128]{1,0:T(8,128)(2,1)} %bitcast.15, bf16[64,128]{1,0:T(8,128)(2,1)} %bitcast.16, s32[1,32]{1,0:T(1,128)} %refs_4_.1, s32[1]{0:T(128)S(6)} %copy.18.refs_5_, s32[1,16]{1,0:T(1,128)} %refs_6_.1, ...), custom_call_target="tpu_custom_call" | custom-call | tf_op jit(solution)/shard_map/pallas_call | solution.py:526
  84.7 1.5 %shard_map.168 = (bf16[32,256]{1,0:T(8,128)(2,1)}, f32[1,32]{1,0:T(1,128)}) custom-call(f32[8,8,256]{2,1,0:T(8,128)} %shard_map.167.parts_ref), custom_call_target="tpu_custom_call" | custom-call | tf_op jit(solution)/shard_map/pallas_call | solution.py:609

commit v3 on v2

--- a/solution.py
+++ b/solution.py
@@ -45,13 +45,14 @@
 ):
     sources, out_ref, held, refs = refs[:16], refs[16], refs[17:33], refs[33:]
     (kv, tail, q_ref, new_ref, tab_ref, plen_ref, tlen_ref, down_ref, ow, resid_ref, mig_ref, gate_ref, up_ref, gain_ref, fg_ref, sw_ref) = held
-    (bias, sbuf, wbuf, s2, r2, xall, perm, sel, hs, gs, r4, auxs, r5, ms, ags, r6, fs, r7, load_sem, w_ssem, w_rsem, wc_ssem, wc_rsem, s2_ssem, s2_rsem, z_ssem, z_rsem, y_ssem, y_rsem, c_ssem, c_rsem, s4_ssem, s4_rsem, s5_ssem, s5_rsem, s6_ssem, s6_rsem, s7_ssem, s7_rsem) = refs
+    (bias, sbuf, wbuf, s2, r2, xall, perm, sel, hs, gs, r4, auxs, r5, ms, ags, r6, fs, r7, load_sem, w_ssem, w_rsem, s2_ssem, s2_rsem, z_ssem, z_rsem, y_ssem, y_rsem, c_ssem, c_rsem, s4_ssem, s4_rsem, s5_ssem, s5_rsem, s6_ssem, s6_rsem, s7_ssem, s7_rsem) = refs
     dp = lax.axis_index("dp")
     b = lax.axis_index("blk")
     c = lax.rem(dp, 2)
     z = lax.rem(lax.div(dp, 2), nz)
     y = lax.div(dp, 2 * nz)
     yc = 2 * y + c
+    x, yh = lax.rem(b, 4), lax.div(b, 4)
     conts = 4 * nz * CONT
     rows = 2 * nz
 
@@ -87,23 +88,21 @@
     for load in loads[2:8]:
         load.wait()
 
-    wbuf[yc, b] = down_ref[...]
-    me16 = y * NB + b
-
-    def w_copy(k):
-        other = lax.rem(me16 + k, 16)
-        return remote(
-            wbuf.at[yc, b],
-            wbuf.at[yc, b],
-            w_ssem.at[k],
-            w_rsem.at[k],
-            dev(lax.div(other, NB), z, c, lax.rem(other, NB)),
-        )
-
-    def wc_copy(i):
-        return remote(
-            wbuf.at[2 * i + c], wbuf.at[2 * i + c], wc_ssem.at[i], wc_rsem.at[i], dev(y, z, 1 - c, b)
-        )
+    wbuf[y, c, yh, x] = down_ref[...]
+    row4 = y * 2 + yh
+
+    def wy_copy(k):
+        other = lax.rem(row4 + k, 4)
+        piece = wbuf.at[y, c, yh, x]
+        return remote(piece, piece, w_ssem.at[k], w_rsem.at[k], dev(lax.div(other, 2), z, c, lax.rem(other, 2) * 4 + x))
+
+    def wx_copy(k):
+        piece = wbuf.at[:, c, :, x]
+        return remote(piece, piece, w_ssem.at[3 + k], w_rsem.at[3 + k], dev(y, z, c, yh * 4 + lax.rem(x + k, 4)))
+
+    def wc_copy():
+        piece = wbuf.at[:, c]
+        return remote(piece, piece, w_ssem.at[7], w_rsem.at[7], dev(y, z, 1 - c, b))
 
     r64, c64 = iota((64, 64), 0), iota((64, 64), 1)
     q_src = (r64 % 16) * 4 + ((r64 // 16) % 2) * 2 + r64 // 32
@@ -112,7 +111,7 @@
     lane = iota((PAGES, 256), 1)
     page_no = iota((PAGES, PAGES), 0) == jnp.broadcast_to(tab_ref[...], (PAGES, PAGES))
     logical = jnp.sum(jnp.where(page_no, iota((PAGES, PAGES), 1), 0), -1, keepdims=True)
-    limit = jnp.broadcast_to(plen_ref[0] - logical * 128, (PAGES, 256))
+    limit = jnp.broadcast_to(plen_ref[0, 0] - logical * 128, (PAGES, 256))
     bias[...] = jnp.where((lane % 2 == 0) & (lane // 2 < limit), 0.0, NEG)
     unit = math.log2(math.e) / math.sqrt(HD)
 
@@ -145,9 +144,6 @@
             t = i * 8 + u
             t_bias = jnp.where((t_lane % 2 == 0) & (t_lane // 2 < tlen_ref[0, t]), 0.0, NEG)
             s_tail = jnp.where(owner == t, s[:, u * 256 : (u + 1) * 256] + t_bias, s_tail)
-
-    pl.semaphore_wait(barrier, 31 + nz - 1)
-    lax.fori_loop(1, 16, lambda k, _: (w_copy(k).start(), 0)[1], 0)
 
     new_cont, new_tok = c64 // 4, (c64 // 2) % 2
     new_ok = (c64 % 2 == 0) & (new_cont == r64 % 16) & (new_tok <= (r64 // 16) % 2)
@@ -173,6 +169,8 @@
     total = jnp.sum(total, -1, keepdims=True) + jnp.sum(w_new, -1, keepdims=True)
     attn = (mixed / total).astype(BF16)
 
+    pl.semaphore_wait(barrier, 31 + nz - 1)
+
     loads[8].wait()
     for i in range(NB):
         cols = slice(i * FB, (i + 1) * FB)
@@ -183,6 +181,7 @@
         return remote(s2.at[other], r2.at[k - 1], s2_ssem.at[k], s2_rsem.at[k], dev(y, z, c, other))
 
     lax.fori_loop(1, NB, lambda k, _: (s2_copy(k).start(), 0)[1], 0)
+    lax.fori_loop(1, 4, lambda k, _: (wy_copy(k).start(), 0)[1], 0)
 
     for load in loads[9:]:
         load.wait()
@@ -276,6 +275,8 @@
     for way in (1, -1):
         z_forward(way, *TREE[0])
     y_forward(1, 0)
+    lax.fori_loop(1, 4, lambda k, _: (wy_copy(k).wait_recv(), 0)[1], 0)
+    lax.fori_loop(1, 4, lambda k, _: (wx_copy(k).start(), 0)[1], 0)
     kids_of = dict(TREE)
     for dist in (2, 5, 1, 4, 3, 6, 7, 8):
         for way in (1, -1):
@@ -311,9 +312,8 @@
     c_copy(1 - y).start()
     res = project(2 * (1 - y) + c, res)
 
-    lax.fori_loop(1, 16, lambda k, _: (w_copy(k).wait_recv(), 0)[1], 0)
-    wc_copy(0).start()
-    wc_copy(1).start()
+    lax.fori_loop(1, 4, lambda k, _: (wx_copy(k).wait_recv(), 0)[1], 0)
+    wc_copy().start()
 
     c_copy(1 - y).wait_recv()
     res = project(2 * (1 - y) + 1 - c, res)
@@ -340,32 +340,38 @@
         ob = lax.rem(b + i, NB)
         return remote(auxs.at[ob], r5.at[b], s5_ssem.at[i], s5_rsem.at[i], dev(y, z, c, ob))
 
-    def serve(i):
-        ob = lax.rem(b + i, NB)
-        g = dot(perm[ob], hs[...].reshape(conts, 512)).astype(BF16)
-        gs[ob] = g[:, :384].reshape(4, rows, 384)
-        return ob, g[:, 384:].reshape(4, rows, 128)
-
-    def aux_rows(ob, squares4):
-        pick = jnp.zeros((rows, 128), BF16)
-        for i in range(4):
-            pick = jnp.where(yc == i, squares4[i], pick)
-        auxs[ob, :rows, :128] = pick
-        auxs[ob, :rows, 128:] = jnp.zeros((rows, 128), BF16)
-
-    def serve_send(i, _):
-        ob, squares4 = serve(i)
-        for j in range(4):
-            s4_copy(i, j).start()
-        aux_rows(ob, squares4)
-        s5_copy(i).start()
+    def serve(pair):
+        lhs = jnp.concatenate([perm[2 * pair], perm[2 * pair + 1]], 0)
+        g = dot(lhs, hs[...].reshape(conts, 512)).astype(BF16)
+        for u in range(2):
+            half = g[u * 4 * rows : (u + 1) * 4 * rows]
+            ob = 2 * pair + u
+            gs[ob] = half[:, :384].reshape(4, rows, 384)
+            squares4 = half[:, 384:].reshape(4, rows, 128)
+            pick = jnp.zeros((rows, 128), BF16)
+            for i in range(4):
+                pick = jnp.where(yc == i, squares4[i], pick)
+            auxs[ob, :rows, :128] = pick
+            auxs[ob, :rows, 128:] = jnp.zeros((rows, 128), BF16)
+
+    def serve_send(step, _):
+        pair = lax.rem(lax.div(b, 2) + step, NB // 2)
+        serve(pair)
+        for u in range(2):
+            away = lax.rem(2 * pair + u - b + NB, NB)
+            for j in range(4):
+                s4_copy(away, j).start()
+            s5_copy(away).start()
         return 0
 
-    lax.fori_loop(1, NB, serve_send, 0)
-    ob, squares4 = serve(0)
+    lax.fori_loop(1, NB // 2, serve_send, 0)
+    serve(lax.div(b, 2))
+    away = lax.rem(1 - 2 * lax.rem(b, 2) + NB, NB)
+    for j in range(4):
+        s4_copy(away, j).start()
+    s5_copy(away).start()
     for j in range(1, 4):
         s4_copy(0, j).start()
-    aux_rows(ob, squares4)
     r4[yc, b] = gs[b, yc]
     r5[b] = auxs[b]
 
@@ -403,15 +409,14 @@
         return jnp.concatenate([h_ab, h_one], 0).astype(BF16)
 
     hids = [hidden(g) for g in range(4)]
-    wc_copy(0).wait_recv()
-    wc_copy(1).wait_recv()
+    wc_copy().wait_recv()
     left = jnp.zeros((nz * 16, FB), F32)
     right = jnp.zeros((nz * 16, FB), F32)
     for g in range(4):
         for j in range(4):
             lhs = dot(spread[j], hids[g]).astype(BF16)[:, :HOLD]
-            left = left + dot(lhs, wbuf[g, 2 * j])
-            right = right + dot(lhs, wbuf[g, 2 * j + 1])
+            left = left + dot(lhs, wbuf[g // 2, g % 2, j // 2, 2 * (j % 2)])
+            right = right + dot(lhs, wbuf[g // 2, g % 2, j // 2, 2 * (j % 2) + 1])
     ms[:, :, :FB] = left.astype(BF16).reshape(nz, 16, FB)
     ms[:, :, FB:] = right.astype(BF16).reshape(nz, 16, FB)
 
@@ -475,9 +480,9 @@
     lax.fori_loop(1, NB, lambda k, _: (s7_copy(k).start(), 0)[1], 0)
     r7[b] = fs[b]
 
-    lax.fori_loop(1, 16, lambda k, _: (w_copy(k).wait_send(), 0)[1], 0)
-    wc_copy(0).wait_send()
-    wc_copy(1).wait_send()
+    lax.fori_loop(1, 4, lambda k, _: (wy_copy(k).wait_send(), 0)[1], 0)
+    lax.fori_loop(1, 4, lambda k, _: (wx_copy(k).wait_send(), 0)[1], 0)
+    wc_copy().wait_send()
     lax.fori_loop(1, NB, lambda k, _: (s2_copy(k).wait_send(), 0)[1], 0)
     for copy in z_waits + y_waits:
         copy.wait_send()
@@ -534,7 +539,7 @@
             pltpu.VMEM((64, HD), BF16),
             pltpu.VMEM((64, HD), BF16),
             pltpu.VMEM((1, PAGES), jnp.int32),
-            pltpu.SMEM((1,), jnp.int32),
+            pltpu.SMEM((1, 1), jnp.int32),
             pltpu.SMEM((1, CONT), jnp.int32),
             pltpu.VMEM((HOLD, FB), BF16),
             pltpu.VMEM((2 * HD, D), BF16),
@@ -547,7 +552,7 @@
             pltpu.VMEM((2, 128), BF16),
             pltpu.VMEM((PAGES, 256), F32),
             pltpu.VMEM((64, PAGES * 256), F32),
-            pltpu.VMEM((4, NB, HOLD, FB), BF16),
+            pltpu.VMEM((2, 2, 2, 4, HOLD, FB), BF16),
             pltpu.VMEM((NB, 32, FB), BF16),
             pltpu.VMEM((NB - 1, 32, FB), BF16),
             pltpu.VMEM((2, 4, nz, CONT, FB), BF16),
@@ -564,10 +569,8 @@
             pltpu.VMEM((NB, 8, FB), F32),
             pltpu.VMEM((NB, 8, FB), F32),
             dma((16,)),
-            dma((16,)),
-            dma((16,)),
-            dma((2,)),
-            dma((2,)),
+            dma((8,)),
+            dma((8,)),
             dma((NB,)),
             dma((NB,)),
             dma((nz,)),
@@ -594,7 +597,7 @@
         queries.reshape(64, HD),
         new_kv.reshape(64, HD),
         page_table,
-        prompt_len,
+        prompt_len.reshape(1, 1),
         tail_len,
         down_w,
         out_w,

time: 86.4 us -> 77.9 us (0.902)
  the two profiles are of different devices: /device:TPU:2 before, /device:TPU:24 now
where the time goes in v3:
time: 77.9 us; the launch traced here: 76.4 us
  Pallas kernels  75.1 us (96%)
  between operations  1.29 us (2%)
    pallas_call x1, Pallas kernels, shards(): pl.pallas_call(functools.partial(kernel, nz), out_shape=jax.ShapeDtypeStr...  73.7 us

profile of v3, /device:TPU:24, one launch (start us, length us, event | category | flops | bytes accessed | tf_op | source)
XLA Modules:
  0.0 76.4 jit_solution(1739391056986434419)
XLA Ops:
  1.3 73.7 %shard_map.167.parts_ref = f32[8,8,256]{2,1,0:T(8,128)} custom-call(bf16[8192,128]{1,0:T(8,128)(2,1)} %bitcast.13, bf16[4096,128]{1,0:T(8,128)(2,1)} %bitcast.14, bf16[64,128]{1,0:T(8,128)(2,1)} %bitcast.17, bf16[64,128]{1,0:T(8,128)(2,1)} %bitcast.18, s32[1,32]{1,0:T(1,128)} %refs_4_.1, s32[1,1]{1,0:T(1,128)} %bitcast.12.refs_5_, s32[1,16]{1,0:T(1,128)} %refs_6_.1, ...), custom_call_target="tpu_custom_call" | custom-call | tf_op jit(solution)/shard_map/pallas_call | solution.py:531
  75.0 1.5 %shard_map.168 = (bf16[32,256]{1,0:T(8,128)(2,1)}, f32[1,32]{1,0:T(1,128)}) custom-call(f32[8,8,256]{2,1,0:T(8,128)} %shard_map.167.parts_ref), custom_call_target="tpu_custom_call" | custom-call | tf_op jit(solution)/shard_map/pallas_call | solution.py:612

commit v4 on v3

--- a/solution.py
+++ b/solution.py
@@ -359,19 +359,22 @@
         serve(pair)
         for u in range(2):
             away = lax.rem(2 * pair + u - b + NB, NB)
-            for j in range(4):
-                s4_copy(away, j).start()
             s5_copy(away).start()
+            s4_copy(away, 1).start()
+            s4_copy(away, 2).start()
         return 0
 
     lax.fori_loop(1, NB // 2, serve_send, 0)
     serve(lax.div(b, 2))
-    away = lax.rem(1 - 2 * lax.rem(b, 2) + NB, NB)
-    for j in range(4):
-        s4_copy(away, j).start()
-    s5_copy(away).start()
-    for j in range(1, 4):
+    sibling = lax.rem(1 - 2 * lax.rem(b, 2) + NB, NB)
+    s5_copy(sibling).start()
+    for j in (1, 2):
+        s4_copy(sibling, j).start()
         s4_copy(0, j).start()
+    for j in (3, 0):
+        lax.fori_loop(0, NB - 1, lambda k, _: (s4_copy(lax.rem(k + 3, NB - 1) + 1, j).start(), 0)[1], 0)
+        if j:
+            s4_copy(0, j).start()
     r4[yc, b] = gs[b, yc]
     r5[b] = auxs[b]
 
@@ -388,7 +391,6 @@
     scale0, scale1 = inverse_rms(0), inverse_rms(1)
     scale_ab = jnp.where(l128 < 96, scale0, scale1)
 
-    lax.fori_loop(1, 32, lambda k, _: (s4_copy(lax.div(k, 4), lax.rem(k, 4)).wait_recv(), 0)[1], 0)
 
     def silu(v):
         return v / (1.0 + jnp.exp(-v))
@@ -408,15 +410,17 @@
         h_one = jnp.where(l128 < 32, pltpu.roll(h_ab, 32, 1), pltpu.roll(h_c, 32, 1))
         return jnp.concatenate([h_ab, h_one], 0).astype(BF16)
 
-    hids = [hidden(g) for g in range(4)]
     wc_copy().wait_recv()
     left = jnp.zeros((nz * 16, FB), F32)
     right = jnp.zeros((nz * 16, FB), F32)
-    for g in range(4):
-        for j in range(4):
-            lhs = dot(spread[j], hids[g]).astype(BF16)[:, :HOLD]
-            left = left + dot(lhs, wbuf[g // 2, g % 2, j // 2, 2 * (j % 2)])
-            right = right + dot(lhs, wbuf[g // 2, g % 2, j // 2, 2 * (j % 2) + 1])
+    for j in (1, 2, 3, 0):
+        lax.fori_loop(0 if j else 1, NB, lambda k, _: (s4_copy(k, j).wait_recv(), 0)[1], 0)
+        g = lax.rem(yc - j + 4, 4)
+        hid = hidden(g)
+        for i in range(4):
+            lhs = dot(spread[i], hid).astype(BF16)[:, :HOLD]
+            left = left + dot(lhs, wbuf[lax.div(g, 2), lax.rem(g, 2), i // 2, 2 * (i % 2)])
+            right = right + dot(lhs, wbuf[lax.div(g, 2), lax.rem(g, 2), i // 2, 2 * (i % 2) + 1])
     ms[:, :, :FB] = left.astype(BF16).reshape(nz, 16, FB)
     ms[:, :, FB:] = right.astype(BF16).reshape(nz, 16, FB)
 

time: 77.9 us -> 74.4 us (0.955)
  Pallas kernels: 75.1 us -> 72.2 us
    pallas_call x1, Pallas kernels: 73.7 us -> 70.7 us  [shards(): pl.pallas_call(functools.partial(kernel, nz), out_shape=jax.ShapeDtypeStr...]
where the time goes in v4:
time: 74.4 us; the launch traced here: 73.5 us
  Pallas kernels  72.2 us (97%)
  between operations  1.29 us (2%)
    pallas_call x1, Pallas kernels, shards(): pl.pallas_call(functools.partial(kernel, nz), out_shape=jax.ShapeDtypeStr...  70.7 us

profile of v4, /device:TPU:24, one launch (start us, length us, event | category | flops | bytes accessed | tf_op | source)
XLA Modules:
  0.0 73.5 jit_solution(7687239812373504072)
XLA Ops:
  1.3 70.7 %shard_map.167.parts_ref = f32[8,8,256]{2,1,0:T(8,128)} custom-call(bf16[8192,128]{1,0:T(8,128)(2,1)} %bitcast.13, bf16[4096,128]{1,0:T(8,128)(2,1)} %bitcast.14, bf16[64,128]{1,0:T(8,128)(2,1)} %bitcast.17, bf16[64,128]{1,0:T(8,128)(2,1)} %bitcast.18, s32[1,32]{1,0:T(1,128)} %refs_4_.1, s32[1,1]{1,0:T(1,128)} %bitcast.12.refs_5_, s32[1,16]{1,0:T(1,128)} %refs_6_.1, ...), custom_call_target="tpu_custom_call" | custom-call | tf_op jit(solution)/shard_map/pallas_call | solution.py:535
  72.0 1.5 %shard_map.168 = (bf16[32,256]{1,0:T(8,128)(2,1)}, f32[1,32]{1,0:T(1,128)}) custom-call(f32[8,8,256]{2,1,0:T(8,128)} %shard_map.167.parts_ref), custom_call_target="tpu_custom_call" | custom-call | tf_op jit(solution)/shard_map/pallas_call | solution.py:616

commit v5 on v4

--- a/solution.py
+++ b/solution.py
@@ -45,7 +45,7 @@
 ):
     sources, out_ref, held, refs = refs[:16], refs[16], refs[17:33], refs[33:]
     (kv, tail, q_ref, new_ref, tab_ref, plen_ref, tlen_ref, down_ref, ow, resid_ref, mig_ref, gate_ref, up_ref, gain_ref, fg_ref, sw_ref) = held
-    (bias, sbuf, wbuf, s2, r2, xall, perm, sel, hs, gs, r4, auxs, r5, ms, ags, r6, fs, r7, load_sem, w_ssem, w_rsem, s2_ssem, s2_rsem, z_ssem, z_rsem, y_ssem, y_rsem, c_ssem, c_rsem, s4_ssem, s4_rsem, s5_ssem, s5_rsem, s6_ssem, s6_rsem, s7_ssem, s7_rsem) = refs
+    (bias, sbuf, wbuf, s2, r2, xall, perm, sel, hs, served, gs, r4, auxs, r5, ms, ags, r6, fs, r7, load_sem, w_ssem, w_rsem, s2_ssem, s2_rsem, z_ssem, z_rsem, y_ssem, y_rsem, c_ssem, c_rsem, s4_ssem, s4_rsem, s5_ssem, s5_rsem, s6_ssem, s6_rsem, s7_ssem, s7_rsem) = refs
     dp = lax.axis_index("dp")
     b = lax.axis_index("blk")
     c = lax.rem(dp, 2)
@@ -275,8 +275,6 @@
     for way in (1, -1):
         z_forward(way, *TREE[0])
     y_forward(1, 0)
-    lax.fori_loop(1, 4, lambda k, _: (wy_copy(k).wait_recv(), 0)[1], 0)
-    lax.fori_loop(1, 4, lambda k, _: (wx_copy(k).start(), 0)[1], 0)
     kids_of = dict(TREE)
     for dist in (2, 5, 1, 4, 3, 6, 7, 8):
         for way in (1, -1):
@@ -285,6 +283,9 @@
                 if dist in kids_of:
                     z_forward(way, dist, kids_of[dist])
                 y_forward(way, dist)
+        if dist == 1:
+            lax.fori_loop(1, 4, lambda k, _: (wy_copy(k).wait_recv(), 0)[1], 0)
+            lax.fori_loop(1, 4, lambda k, _: (wx_copy(k).start(), 0)[1], 0)
 
     e_lane = iota((FB, 128), 1)
     e_first = onehot((e_lane == 0) | (e_lane == 2))
@@ -307,13 +308,23 @@
     res = project(yc, jnp.zeros((128, FB), F32))
     c_copy(y).wait_recv()
     res = project(2 * y + 1 - c, res)
+
+    half = 2 * nz * CONT
+
+    def share(pair, side):
+        cols = pl.ds(pl.multiple_of(side * half, half), half)
+        lhs = jnp.concatenate([perm[2 * pair, :, cols], perm[2 * pair + 1, :, cols]], 0)
+        return dot(lhs, hs[pl.ds(2 * side, 2)].reshape(half, 512))
+
+    def first_share(pair, _):
+        served[pair] = share(pair, y)
+        return 0
+
+    lax.fori_loop(0, NB // 2, first_share, 0)
     for copy in y_waits:
         copy.wait_recv()
     c_copy(1 - y).start()
     res = project(2 * (1 - y) + c, res)
-
-    lax.fori_loop(1, 4, lambda k, _: (wx_copy(k).wait_recv(), 0)[1], 0)
-    wc_copy().start()
 
     c_copy(1 - y).wait_recv()
     res = project(2 * (1 - y) + 1 - c, res)
@@ -341,13 +352,12 @@
         return remote(auxs.at[ob], r5.at[b], s5_ssem.at[i], s5_rsem.at[i], dev(y, z, c, ob))
 
     def serve(pair):
-        lhs = jnp.concatenate([perm[2 * pair], perm[2 * pair + 1]], 0)
-        g = dot(lhs, hs[...].reshape(conts, 512)).astype(BF16)
+        g = (served[pair] + share(pair, 1 - y)).astype(BF16)
         for u in range(2):
-            half = g[u * 4 * rows : (u + 1) * 4 * rows]
+            quads = g[u * 4 * rows : (u + 1) * 4 * rows]
             ob = 2 * pair + u
-            gs[ob] = half[:, :384].reshape(4, rows, 384)
-            squares4 = half[:, 384:].reshape(4, rows, 128)
+            gs[ob] = quads[:, :384].reshape(4, rows, 384)
+            squares4 = quads[:, 384:].reshape(4, rows, 128)
             pick = jnp.zeros((rows, 128), BF16)
             for i in range(4):
                 pick = jnp.where(yc == i, squares4[i], pick)
@@ -371,6 +381,8 @@
     for j in (1, 2):
         s4_copy(sibling, j).start()
         s4_copy(0, j).start()
+    lax.fori_loop(1, 4, lambda k, _: (wx_copy(k).wait_recv(), 0)[1], 0)
+    wc_copy().start()
     for j in (3, 0):
         lax.fori_loop(0, NB - 1, lambda k, _: (s4_copy(lax.rem(k + 3, NB - 1) + 1, j).start(), 0)[1], 0)
         if j:
@@ -563,6 +575,7 @@
             pltpu.VMEM((NB, 4 * rows, conts), BF16),
             pltpu.VMEM((2, 4, 128, nz * CONT), BF16),
             pltpu.VMEM((4, nz * CONT, 512), BF16),
+            pltpu.VMEM((NB // 2, 8 * rows, 512), F32),
             pltpu.VMEM((NB, 4, rows, 384), BF16),
             pltpu.VMEM((4, NB, rows, 384), BF16),
             pltpu.VMEM((NB, rows + 16, FB), BF16),

time: 74.4 us -> 74.3 us (level)
  no operation moved by 1% of the time
where the time goes in v5:
time: 74.3 us; the launch traced here: 74.1 us
  Pallas kernels  72.8 us (98%)
  between operations  1.29 us (2%)
    pallas_call x1, Pallas kernels, shards(): pl.pallas_call(functools.partial(kernel, nz), out_shape=jax.ShapeDtypeStr...  71.3 us

profile of v5, /device:TPU:24, one launch (start us, length us, event | category | flops | bytes accessed | tf_op | source)
XLA Modules:
  0.0 74.1 jit_solution(10555266102113609114)
XLA Ops:
  1.3 71.3 %shard_map.167.parts_ref = f32[8,8,256]{2,1,0:T(8,128)} custom-call(bf16[8192,128]{1,0:T(8,128)(2,1)} %bitcast.13, bf16[4096,128]{1,0:T(8,128)(2,1)} %bitcast.14, bf16[64,128]{1,0:T(8,128)(2,1)} %bitcast.17, bf16[64,128]{1,0:T(8,128)(2,1)} %bitcast.18, s32[1,32]{1,0:T(1,128)} %refs_4_.1, s32[1,1]{1,0:T(1,128)} %bitcast.12.refs_5_, s32[1,16]{1,0:T(1,128)} %refs_6_.1, ...), custom_call_target="tpu_custom_call" | custom-call | tf_op jit(solution)/shard_map/pallas_call | solution.py:547
  72.6 1.5 %shard_map.168 = (bf16[32,256]{1,0:T(8,128)(2,1)}, f32[1,32]{1,0:T(1,128)}) custom-call(f32[8,8,256]{2,1,0:T(8,128)} %shard_map.167.parts_ref), custom_call_target="tpu_custom_call" | custom-call | tf_op jit(solution)/shard_map/pallas_call | solution.py:629

commit v6 on v5

--- a/solution.py
+++ b/solution.py
@@ -45,7 +45,7 @@
 ):
     sources, out_ref, held, refs = refs[:16], refs[16], refs[17:33], refs[33:]
     (kv, tail, q_ref, new_ref, tab_ref, plen_ref, tlen_ref, down_ref, ow, resid_ref, mig_ref, gate_ref, up_ref, gain_ref, fg_ref, sw_ref) = held
-    (bias, sbuf, wbuf, s2, r2, xall, perm, sel, hs, served, gs, r4, auxs, r5, ms, ags, r6, fs, r7, load_sem, w_ssem, w_rsem, s2_ssem, s2_rsem, z_ssem, z_rsem, y_ssem, y_rsem, c_ssem, c_rsem, s4_ssem, s4_rsem, s5_ssem, s5_rsem, s6_ssem, s6_rsem, s7_ssem, s7_rsem) = refs
+    (bias, sbuf, wbuf, s2, r2, xall, perm, sel, hs, served, gs, r4, auxb, auxs, r5, ms, ags, r6, fs, r7, load_sem, w_ssem, w_rsem, s2_ssem, s2_rsem, z_ssem, z_rsem, y_ssem, y_rsem, c_ssem, c_rsem, s4_ssem, s4_rsem, s5_ssem, s5_rsem, s6_ssem, s6_rsem, s7_ssem, s7_rsem) = refs
     dp = lax.axis_index("dp")
     b = lax.axis_index("blk")
     c = lax.rem(dp, 2)
@@ -227,7 +227,8 @@
     for n in range(2):
         picked = dot(
             onehot(
-                (place < 4)
+                (place >= 4)
+                & (place < 12)
                 & (place % 2 == n)
                 & (sel_c == (sel_r // 16) * rows + z * 2 + (place // 2) % 2)
             ),
@@ -331,11 +332,13 @@
 
     fg = fg_ref[...].astype(F32)
     sw = sw_ref[...].astype(F32)
-    a_row = iota((128, FB), 0) % 16
-    res = jnp.where(a_row == 4, jnp.concatenate([fg[0:1], fg[1:2]], 1), res)
-    res = jnp.where(a_row == 5, jnp.concatenate([sw[0:1], sw[1:2]], 1), res).astype(BF16)
+    a_row = iota((128, 128), 0) % 16
+    aux = jnp.where(a_row < 8, res[:, :128], res[:, 128:])
+    for i, line in enumerate((fg[0:1], fg[1:2], sw[0:1], sw[1:2])):
+        aux = jnp.where(a_row == 12 + i, line, aux)
     for i in range(NB):
-        auxs[i, rows : rows + 16, :] = res[i * 16 : (i + 1) * 16]
+        auxb[i] = aux[i * 16 : (i + 1) * 16]
+    four = onehot((iota((16, 128), 0) == iota((16, 128), 1)) & (iota((16, 128), 0) < 4))
 
     def s4_copy(i, j):
         ob, oyc = lax.rem(b + i, NB), lax.rem(yc + j, 4)
@@ -357,12 +360,10 @@
             quads = g[u * 4 * rows : (u + 1) * 4 * rows]
             ob = 2 * pair + u
             gs[ob] = quads[:, :384].reshape(4, rows, 384)
-            squares4 = quads[:, 384:].reshape(4, rows, 128)
-            pick = jnp.zeros((rows, 128), BF16)
-            for i in range(4):
-                pick = jnp.where(yc == i, squares4[i], pick)
-            auxs[ob, :rows, :128] = pick
-            auxs[ob, :rows, 128:] = jnp.zeros((rows, 128), BF16)
+            squares4 = quads[:, 384:]
+            if 4 * rows < 128:
+                squares4 = jnp.concatenate([squares4, jnp.zeros((128 - 4 * rows, 128), BF16)], 0)
+            auxs[ob] = (auxb[ob] + dot_nt(four, squares4)).astype(BF16)
 
     def serve_send(step, _):
         pair = lax.rem(lax.div(b, 2) + step, NB // 2)
@@ -391,14 +392,16 @@
     r5[b] = auxs[b]
 
     lax.fori_loop(1, NB, lambda k, _: (s5_copy(k).wait_recv(), 0)[1], 0)
-    stats = r5[0, :rows, :128].astype(F32)
+    stats = r5[0].astype(F32)
     for i in range(1, NB):
-        stats = stats + r5[i, :rows, :128].astype(F32)
+        stats = stats + r5[i].astype(F32)
     l128 = iota((rows, 128), 1)
+    mine = l128 == yc * rows + iota((rows, 128), 0)
 
     def inverse_rms(n):
-        picked = jnp.where(l128 % 2 == n, jnp.where(l128 < 4, stats, 0.0), 0.0)
-        return lax.rsqrt(jnp.sum(picked, -1, keepdims=True) / D + EPS)
+        line = stats[n : n + 1] + stats[n + 2 : n + 3]
+        column = jnp.sum(jnp.where(mine, jnp.broadcast_to(line, (rows, 128)), 0.0), -1, keepdims=True)
+        return lax.rsqrt(column / D + EPS)
 
     scale0, scale1 = inverse_rms(0), inverse_rms(1)
     scale_ab = jnp.where(l128 < 96, scale0, scale1)
@@ -457,10 +460,11 @@
             [jnp.concatenate([pick(2 * j), pick(2 * j + 1)], 1) for j in range(4)], 0
         )
 
-    resid4 = gathered(lambda i: r5[i, rows : rows + 16, :].astype(F32)[0:4])
+    got = [r5[i].astype(F32) for i in range(NB)]
+    resid4 = gathered(lambda i: jnp.concatenate([got[i][4:8], got[i][8:12]], 1))
     weight4 = gathered(
         lambda i: jnp.broadcast_to(
-            r5[i, rows : rows + 16, :].astype(F32)[4:5] * r5[i, rows : rows + 16, :].astype(F32)[5:6], (4, FB)
+            jnp.concatenate([got[i][12:13] * got[i][14:15], got[i][13:14] * got[i][15:16]], 1), (4, FB)
         )
     )
 
@@ -578,8 +582,9 @@
             pltpu.VMEM((NB // 2, 8 * rows, 512), F32),
             pltpu.VMEM((NB, 4, rows, 384), BF16),
             pltpu.VMEM((4, NB, rows, 384), BF16),
-            pltpu.VMEM((NB, rows + 16, FB), BF16),
-            pltpu.VMEM((NB, rows + 16, FB), BF16),
+            pltpu.VMEM((NB, 16, 128), F32),
+            pltpu.VMEM((NB, 16, 128), BF16),
+            pltpu.VMEM((NB, 16, 128), BF16),
             pltpu.VMEM((nz, 16, 512), BF16),
             pltpu.VMEM((2, len(TREE) - 1, 16, 512), BF16),
             pltpu.VMEM((nz, 16, 512), BF16),

time: 74.3 us -> 72.8 us (0.980)
  Pallas kernels: 72.8 us -> 70.9 us
    pallas_call x1, Pallas kernels: 71.3 us -> 69.4 us  [shards(): pl.pallas_call(functools.partial(kernel, nz), out_shape=jax.ShapeDtypeStr...]
where the time goes in v6:
time: 72.8 us; the launch traced here: 72.2 us
  Pallas kernels  70.9 us (97%)
  between operations  1.29 us (2%)
    pallas_call x1, Pallas kernels, shards(): pl.pallas_call(functools.partial(kernel, nz), out_shape=jax.ShapeDtypeStr...  69.4 us

profile of v6, /device:TPU:24, one launch (start us, length us, event | category | flops | bytes accessed | tf_op | source)
XLA Modules:
  0.0 72.2 jit_solution(14219596710772490481)
XLA Ops:
  1.3 69.4 %shard_map.167.parts_ref = f32[8,8,256]{2,1,0:T(8,128)} custom-call(bf16[8192,128]{1,0:T(8,128)(2,1)} %bitcast.13, bf16[4096,128]{1,0:T(8,128)(2,1)} %bitcast.14, bf16[64,128]{1,0:T(8,128)(2,1)} %bitcast.17, bf16[64,128]{1,0:T(8,128)(2,1)} %bitcast.18, s32[1,32]{1,0:T(1,128)} %refs_4_.1, s32[1,1]{1,0:T(1,128)} %bitcast.12.refs_5_, s32[1,16]{1,0:T(1,128)} %refs_6_.1, ...), custom_call_target="tpu_custom_call" | custom-call | tf_op jit(solution)/shard_map/pallas_call | solution.py:551
  70.7 1.5 %shard_map.168 = (bf16[32,256]{1,0:T(8,128)(2,1)}, f32[1,32]{1,0:T(1,128)}) custom-call(f32[8,8,256]{2,1,0:T(8,128)} %shard_map.167.parts_ref), custom_call_target="tpu_custom_call" | custom-call | tf_op jit(solution)/shard_map/pallas_call | solution.py:634

commit v7 on v6

--- a/solution.py
+++ b/solution.py
@@ -79,7 +79,14 @@
         return 0
 
     loads = [pltpu.make_async_copy(sources[i], held[i], load_sem.at[i]) for i in range(16)]
-    for load in loads:
+    piece = PAGES * 64
+    kv_loads = [
+        pltpu.make_async_copy(
+            sources[0].at[pl.ds(i * piece, piece)], held[0].at[pl.ds(i * piece, piece)], load_sem.at[16 + i]
+        )
+        for i in range(4)
+    ]
+    for load in loads[2:8] + kv_loads + loads[1:2] + loads[8:]:
         load.start()
 
     lax.fori_loop(1, 32, greet_plane, 0)
@@ -125,9 +132,9 @@
             [pltpu.roll(w[:, i * 128 : (i + 1) * 128], 1, 1) for i in range(w.shape[1] // 128)], 1
         ).astype(BF16)
 
-    loads[0].wait()
     best = jnp.full((64, 128), NEG, F32)
     for i in range(PAGES // 8):
+        kv_loads[i].wait()
         s = dot_nt(q, kv[i * 2048 : (i + 1) * 2048, :])
         for u in range(8):
             l = i * 8 + u
@@ -321,11 +328,12 @@
         served[pair] = share(pair, y)
         return 0
 
-    lax.fori_loop(0, NB // 2, first_share, 0)
+    lax.fori_loop(0, NB // 4, first_share, 0)
     for copy in y_waits:
         copy.wait_recv()
     c_copy(1 - y).start()
     res = project(2 * (1 - y) + c, res)
+    lax.fori_loop(NB // 4, NB // 2, first_share, 0)
 
     c_copy(1 - y).wait_recv()
     res = project(2 * (1 - y) + 1 - c, res)
@@ -590,7 +598,7 @@
             pltpu.VMEM((nz, 16, 512), BF16),
             pltpu.VMEM((NB, 8, FB), F32),
             pltpu.VMEM((NB, 8, FB), F32),
-            dma((16,)),
+            dma((20,)),
             dma((8,)),
             dma((8,)),
             dma((NB,)),

time: 72.8 us -> 72.8 us (level); the launches traced: 72.2 us -> 71.4 us
  Pallas kernels: 70.9 us -> 70.1 us
    pallas_call x1, Pallas kernels: 69.4 us -> 68.7 us  [shards(): pl.pallas_call(functools.partial(kernel, nz), out_shape=jax.ShapeDtypeStr...]
where the time goes in v7:
time: 72.8 us; the launch traced here: 71.4 us
  Pallas kernels  70.1 us (96%)
  between operations  1.29 us (2%)
    pallas_call x1, Pallas kernels, shards(): pl.pallas_call(functools.partial(kernel, nz), out_shape=jax.ShapeDtypeStr...  68.7 us

profile of v7, /device:TPU:24, one launch (start us, length us, event | category | flops | bytes accessed | tf_op | source)
XLA Modules:
  0.0 71.4 jit_solution(9358812961450439228)
XLA Ops:
  1.3 68.7 %shard_map.167.parts_ref = f32[8,8,256]{2,1,0:T(8,128)} custom-call(bf16[8192,128]{1,0:T(8,128)(2,1)} %bitcast.13, bf16[4096,128]{1,0:T(8,128)(2,1)} %bitcast.14, bf16[64,128]{1,0:T(8,128)(2,1)} %bitcast.17, bf16[64,128]{1,0:T(8,128)(2,1)} %bitcast.18, s32[1,32]{1,0:T(1,128)} %refs_4_.1, s32[1,1]{1,0:T(1,128)} %bitcast.12.refs_5_, s32[1,16]{1,0:T(1,128)} %refs_6_.1, ...), custom_call_target="tpu_custom_call" | custom-call | tf_op jit(solution)/shard_map/pallas_call | solution.py:559
  70.0 1.5 %shard_map.168 = (bf16[32,256]{1,0:T(8,128)(2,1)}, f32[1,32]{1,0:T(1,128)}) custom-call(f32[8,8,256]{2,1,0:T(8,128)} %shard_map.167.parts_ref), custom_call_target="tpu_custom_call" | custom-call | tf_op jit(solution)/shard_map/pallas_call | solution.py:642
